TPU v7x, 256 devices: a whole 4x4x8 slice. The times are simulated.
256 devices in a mesh: rows: 32 (over z, x), cols: 8 (over y, core).
Axes of the slice: x: 4, y: 4, z: 8, core: 2. Of those that a mesh axis runs over, the one named last changes fastest.
Arguments:
- block_values: bfloat16 [256, 256, 128, 128], P('rows', 'cols')
- block_columns: int32 [256, 256], P('rows', 'cols'), may hold values from 0 to 1023, as said below
- row_counts: int32 [256, 8], P('rows', 'cols'), may hold values from 1 to 32, as said below
- sketch: bfloat16 [1048576, 256], P(('rows', 'cols')), may hold values from -6 to 6
Outputs:
- basis: float32 [32768, 256], P(('rows', 'cols'))
- triangle: float32 [256, 256], replicated
Inputs may be any that keep to these rules, and one draw needn't show every extreme that they name: row_counts[b, c] counts the live slots among slots c * 32 to c * 32 + 31 of block-row b; some entry equals 32. `block_columns`: take the 8 x 32 slots of one index of rows and one column group c; among them at most 12 name block-columns j with the same j // 32, and in every such set some j // 32 is named by exactly 12 slots.
All inputs are finite; a program needn't handle non-finite values.
Results may differ from a plain program's by a relative error of at most 0.0003.
Values may be sent and summed in bfloat16 or wider, within the bound.
No kernel may reach another device: no remote copies, remote signals or barrier semaphores. Data moves between devices by JAX's collectives and lax.ppermute only.
A program may use at most 128 MiB of HBM per device.

v0:
```python
import functools

import jax
import jax.numpy as jnp
from jax import lax
from jax.experimental import pallas as pl
from jax.experimental.pallas import tpu as pltpu
from jax.sharding import Mesh
from jax.sharding import PartitionSpec as P

NZ, NX, NY, NC = 8, 4, 4, 2
CAP = 12
FULL = NZ * CAP
FIRST = 72
REST = FULL - FIRST
BR, S, BS, K = 8, 32, 128, 256
BPD = 32
ENTRIES = NX * CAP
ROWS = NX * BR
HIGH = lax.Precision.HIGHEST


def ring(n, shift):
    return [(i, (i + shift) % n) for i in range(n)]


def split_kernel(x_ref, near, far, buf, isem, osem):
    step = BPD // 4
    loads, stores = [], []
    for c in range(4):
        out = (near, far)[c // 2].at[pl.ds(c % 2 * step, step)]
        loads.append(pltpu.make_async_copy(x_ref.at[pl.ds(c * step, step)], buf.at[c], isem.at[c]))
        stores.append(pltpu.make_async_copy(buf.at[c], out, osem.at[c]))
    for c in loads:
        c.start()
    for load, store in zip(loads, stores):
        load.wait()
        store.start()
    for c in stores:
        c.wait()


def split(blocks):
    half = jax.ShapeDtypeStruct((BPD // 2, BS, K), jnp.bfloat16)
    anyspec = pl.BlockSpec(memory_space=pl.ANY)
    return pl.pallas_call(
        split_kernel,
        out_shape=[half, half],
        in_specs=[anyspec],
        out_specs=[anyspec, anyspec],
        scratch_shapes=[
            pltpu.VMEM((4, BPD // 4, BS, K), jnp.bfloat16),
            pltpu.SemaphoreType.DMA((4,)),
            pltpu.SemaphoreType.DMA((4,)),
        ],
        compiler_params=pltpu.CompilerParams(vmem_limit_bytes=60 << 20),
        cost_estimate=pl.CostEstimate(
            flops=0, bytes_accessed=2 * BPD * BS * K * 2, transcendentals=0
        ),
        name="split",
    )(blocks)


def pack_kernel(n, index, values, *refs):
    outs, (buf, gsem, osem) = refs[:n], refs[n:]
    for m in range(n):

        def fetch(i, carry, m=m):
            pltpu.make_async_copy(
                values.at[index[m * FIRST + i]], buf.at[m, i], gsem.at[m]
            ).start()
            return carry

        lax.fori_loop(0, FIRST, fetch, 0, unroll=8)
    stores = []
    for m in range(n):
        pltpu.make_async_copy(values.at[pl.ds(0, FIRST)], buf.at[m], gsem.at[m]).wait()
        stores.append(pltpu.make_async_copy(buf.at[m], outs[m], osem.at[m]))
        stores[-1].start()
    for c in stores:
        c.wait()


def pack(index, values):
    n = index.shape[0]
    anyspec = pl.BlockSpec(memory_space=pl.ANY)
    return pl.pallas_call(
        functools.partial(pack_kernel, n),
        out_shape=[jax.ShapeDtypeStruct((FIRST, BS, BS), jnp.bfloat16)] * n,
        grid_spec=pltpu.PrefetchScalarGridSpec(
            num_scalar_prefetch=1,
            grid=(1,),
            in_specs=[anyspec],
            out_specs=[anyspec] * n,
            scratch_shapes=[
                pltpu.VMEM((n, FIRST, BS, BS), jnp.bfloat16),
                pltpu.SemaphoreType.DMA((n,)),
                pltpu.SemaphoreType.DMA((n,)),
            ],
        ),
        compiler_params=pltpu.CompilerParams(vmem_limit_bytes=16 << 20),
        cost_estimate=pl.CostEstimate(
            flops=0, bytes_accessed=2 * n * FIRST * BS * BS * 2, transcendentals=0
        ),
    )(index.reshape(-1), values)


def products_kernel(ds, halves, window, first, *refs):
    refs = list(refs)
    tbl, num = refs[0], refs[1]
    whole = window == FULL
    vals = refs[2 : 2 + NX]
    pos = 2 + NX
    if whole:
        more = refs[pos : pos + NX]
        pos += NX
    tabs = []
    for h in halves:
        tabs.append(refs[pos : pos + h])
        pos += h
    if not first:
        pos += 2
    rows = refs[pos : pos + 2]
    vb, tb, vsem, tsem, msem = refs[pos + 2 :]
    size = min(window, FIRST)
    loads = [
        pltpu.make_async_copy(
            vals[dx].at[pl.ds(0, size)], vb.at[dx, pl.ds(0, size)], vsem.at[dx]
        )
        for dx in range(NX)
    ]
    for i in range(len(ds)):
        part = BPD // halves[i]
        loads += [
            pltpu.make_async_copy(tabs[i][h], tb.at[i, pl.ds(h * part, part)], tsem.at[i, h])
            for h in range(halves[i])
        ]
    for c in loads:
        c.start()
    vb[0, window] = jnp.zeros((BS, BS), jnp.bfloat16)
    for h in range(2):
        if first:
            rows[h][...] = jnp.zeros_like(rows[h])
    if whole:

        @pl.when(num[2 * NZ] > FIRST)
        def _():
            for dx in range(NX):
                c = pltpu.make_async_copy(more[dx], vb.at[dx, pl.ds(FIRST, REST)], msem)
                c.start()
                c.wait()

    for c in loads:
        c.wait()

    def one_distance(i, carry):
        d = ds[0]
        for k in range(1, len(ds)):
            d = jnp.where(i == k, ds[k], d)
        for h in range(2):
            which = 2 * d + h

            def step(j, carry, h=h, which=which):
                for u in range(4):
                    entry = tbl[which * ENTRIES + j * 4 + u]
                    p = jnp.minimum(jnp.bitwise_and(entry, 127), window)
                    dx = jnp.bitwise_and(lax.shift_right_logical(entry, 7), 3)
                    t = jnp.bitwise_and(lax.shift_right_logical(entry, 9), 31)
                    row = lax.shift_right_logical(entry, 14)
                    rows[h][row] += jnp.dot(
                        vb[dx, p], tb[i, t], preferred_element_type=jnp.float32
                    )
                return carry

            lax.fori_loop(0, (num[which] + 3) // 4, step, 0)
        return carry

    lax.fori_loop(0, len(ds), one_distance, 0)


def products(ds, window, tbl, num, vals, more, tabs, prev):
    halves = tuple(len(t) for t in tabs)
    first = prev is None
    args = list(vals) + (list(more) if window == FULL else [])
    args += [a for t in tabs for a in t]
    smem = pl.BlockSpec(memory_space=pltpu.SMEM)
    vmem = pl.BlockSpec(memory_space=pltpu.VMEM)
    anyspec = pl.BlockSpec(memory_space=pl.ANY)
    specs = [smem, smem] + [anyspec] * len(args)
    aliases = {}
    if not first:
        aliases = {len(specs): 0, len(specs) + 1: 1}
        args += list(prev)
        specs += [vmem, vmem]
    nd = len(ds)
    return pl.pallas_call(
        functools.partial(products_kernel, ds, halves, window, first),
        out_shape=[jax.ShapeDtypeStruct((ROWS // 2, BS, K), jnp.float32)] * 2,
        in_specs=specs,
        out_specs=[vmem, vmem],
        scratch_shapes=[
            pltpu.VMEM((NX, window + 1, BS, BS), jnp.bfloat16),
            pltpu.VMEM((nd, BPD, BS, K), jnp.bfloat16),
            pltpu.SemaphoreType.DMA((NX,)),
            pltpu.SemaphoreType.DMA((nd, 2)),
            pltpu.SemaphoreType.DMA,
        ],
        input_output_aliases=aliases,
        compiler_params=pltpu.CompilerParams(vmem_limit_bytes=40 << 20),
        cost_estimate=pl.CostEstimate(
            flops=nd * 20 * 2 * BS * BS * K,
            bytes_accessed=nd * BPD * BS * K * 2 + NX * window * BS * BS * 2,
            transcendentals=0,
        ),
    )(tbl, num, *args)


HB = 64


def factor_block(d):
    groups = [d[8 * g : 8 * g + 8, :] for g in range(8)]
    sub = lax.broadcasted_iota(jnp.int32, (8, 128), 0)
    for p in range(8):
        r = groups[p]
        cols = [jnp.broadcast_to(r[:, 8 * p + k : 8 * p + k + 1], (8, 128)) for k in range(8)]
        a = [
            [jnp.broadcast_to(cols[k][i : i + 1, :], (8, 128)) if i <= k else None for k in range(8)]
            for i in range(8)
        ]
        rs = [None] * 8
        rows = []
        for i in range(8):
            rs[i] = lax.rsqrt(a[i][i])
            for k in range(i + 1, 8):
                a[i][k] = a[i][k] * rs[i]
            for k in range(i + 1, 8):
                for l in range(k, 8):
                    a[k][l] = a[k][l] - a[i][k] * a[i][l]
            row = jnp.broadcast_to(r[i : i + 1, :], (8, 128))
            for k in range(i):
                row = row - a[k][i] * rows[k]
            rows.append(row * rs[i])
        for g in range(p + 1, 8):
            cur = groups[g]
            mult = []
            for i in range(8):
                m = jnp.broadcast_to(cur[:, 8 * p + i : 8 * p + i + 1], (8, 128))
                for k in range(i):
                    m = m - mult[k] * a[k][i]
                mult.append(m * rs[i])
            for i in range(8):
                cur = cur - mult[i] * rows[i]
            groups[g] = cur
        new = rows[0]
        for i in range(1, 8):
            new = jnp.where(sub == i, rows[i], new)
        groups[p] = new
    return jnp.concatenate(groups, axis=0)


def factor_kernel(g_ref, xt_ref, tri_ref, basis_ref, a_ref, w_ref):
    a_ref[...] = g_ref[...]
    w_ref[...] = xt_ref[...]
    lane = lax.broadcasted_iota(jnp.int32, (HB, 128), 1)
    srow = lax.broadcasted_iota(jnp.int32, (HB, 128), 0)
    eye = jnp.where(lane - HB == srow, 1.0, 0.0).astype(jnp.float32)
    low = lane < HB
    rown = lax.broadcasted_iota(jnp.int32, (HB, K), 0)
    coln = lax.broadcasted_iota(jnp.int32, (HB, K), 1)
    for b in range(K // HB):
        lo, hi = b * HB, (b + 1) * HB
        tile = a_ref[lo:hi, 128 * (b // 2) : 128 * (b // 2) + 128]
        if b % 2:
            tile = pltpu.roll(tile, HB, 1)
        res = factor_block(jnp.where(low, tile, eye))
        inv = jnp.where(low, 0.0, res)
        left = lo // 128 * 128
        zero = jnp.zeros((HB, K - left + BS), jnp.float32)
        both = jnp.concatenate([a_ref[lo:hi, left:], w_ref[lo:hi, :]], axis=1)
        out = jnp.dot(
            inv,
            jnp.concatenate([zero, both], axis=0),
            precision=HIGH,
            preferred_element_type=jnp.float32,
        )
        upper = jnp.where((coln >= rown + lo)[:, left:], out[:, : K - left], 0.0)
        if left:
            tri_ref[lo:hi, :left] = jnp.zeros((HB, left), jnp.float32)
        tri_ref[lo:hi, left:] = upper
        w_ref[lo:hi, :] = out[:, K - left :]
        if hi < K:
            rest = hi // 128 * 128
            part = upper[:, rest - left :]
            new = jnp.concatenate([part, out[:, K - left :]], axis=1)
            upd = lax.dot_general(
                part,
                new,
                (((0,), (0,)), ((), ())),
                precision=HIGH,
                preferred_element_type=jnp.float32,
            )
            a_ref[hi:, rest:] = a_ref[hi:, rest:] - upd[hi - rest :, : K - rest]
            w_ref[hi:, :] = w_ref[hi:, :] - upd[hi - rest :, K - rest :]
    basis_ref[...] = w_ref[...].T


def factor(gram, xt):
    vm = pl.BlockSpec(memory_space=pltpu.VMEM)
    return pl.pallas_call(
        factor_kernel,
        out_shape=[
            jax.ShapeDtypeStruct((K, K), jnp.float32),
            jax.ShapeDtypeStruct((BS, K), jnp.float32),
        ],
        in_specs=[vm, vm],
        out_specs=[vm, vm],
        scratch_shapes=[pltpu.VMEM((K, K), jnp.float32), pltpu.VMEM((K, BS), jnp.float32)],
        name="factor",
    )(gram, xt)


def hand_on_kernel(x_ref, o_ref):
    o_ref[...] = x_ref[...]


def hand_on(x):
    vm = pl.BlockSpec(memory_space=pltpu.VMEM)
    return pl.pallas_call(
        hand_on_kernel,
        out_shape=jax.ShapeDtypeStruct(x.shape, x.dtype),
        in_specs=[vm],
        out_specs=vm,
        name="hand_on",
    )(x)


def rank_in_group(group, order):
    n = group.shape[-1]
    key = order * n + jnp.arange(n, dtype=jnp.int32)
    same = group[..., None, :] == group[..., :, None]
    before = key[..., None, :] < key[..., :, None]
    return jnp.sum((same & before).astype(jnp.int32), axis=-1)


def distance_order(d):
    return jnp.where(d == 4, 0, jnp.where(d == 3, 1, jnp.where(d == 5, 2, d + 3)))


def one_device(block_values, block_columns, row_counts, sketch):
    z, x, core = lax.axis_index("z"), lax.axis_index("x"), lax.axis_index("core")
    blocks = split(sketch.reshape(BPD, BS, K))
    have = {0: [sketch.reshape(BPD, BS, K)]}
    fwd = {1: [lax.ppermute(blocks[h], "z", ring(NZ, 1)) for h in range(2)]}
    bwd = {1: [lax.ppermute(blocks[h], "z", ring(NZ, -1)) for h in range(2)]}

    slots = BR * S
    live = jnp.arange(S, dtype=jnp.int32)[None, :] < row_counts
    meta = jnp.where(live, block_columns, -1).reshape(slots)
    ids = jnp.arange(slots, dtype=jnp.int32)
    own = meta // BPD
    dist_z = (own // NX - z) % NZ
    dist_x = jnp.where(meta < 0, NX, (own % NX - x) % NX)
    place = dist_x * FULL + rank_in_group(dist_x, distance_order(dist_z))
    spots = jnp.arange(NX * FULL, dtype=jnp.int32)
    wanted = jnp.sum(jnp.where(place[:, None] == spots[None, :], ids[:, None], 0), axis=0)
    wanted = wanted.reshape(NX, FULL)
    flat_values = block_values.reshape(slots, BS, BS)
    metas = [meta.reshape(2, 128)]
    for dx in range(1, NX):
        metas.append(lax.ppermute(metas[0], "x", ring(NX, dx)))
    wanted, metas = lax.optimization_barrier((wanted, metas))
    vals = [*pack(wanted[:1, :FIRST], flat_values), *pack(wanted[1:, :FIRST], flat_values)]
    for dx in range(1, NX):
        vals[dx] = lax.ppermute(vals[dx], "x", ring(NX, dx))

    for step in range(1, 5):
        if step > 1:
            fwd[step] = [None, None]
            bwd[step] = [None, None]
            for h in range(2):
                if step < 4 or h == 0:
                    fwd[step][h] = lax.ppermute(fwd[step - 1][h], "z", ring(NZ, 1))
                if step < 4 or h == 1:
                    bwd[step][h] = lax.ppermute(bwd[step - 1][h], "z", ring(NZ, -1))
        if step < 4:
            have[NZ - step] = fwd[step]
            have[step] = bwd[step]
        else:
            have[4] = [fwd[4][0], bwd[4][1]]

    metas[0] = hand_on(metas[0])
    got = jnp.stack([m.reshape(slots) for m in metas])
    own = got // BPD
    shift = jnp.arange(NX, dtype=jnp.int32)[:, None]
    source = (x - shift) % NX
    towards = jnp.where(got < 0, NX, own % NX)
    match = towards == x
    dist = (own // NX - z) % NZ
    place = rank_in_group(towards, distance_order(dist))
    block_row = (ids // S)[None, :]
    group = jnp.where(match, 2 * dist + ((block_row % NC) ^ core), 2 * NZ)
    rank = rank_in_group(group, jnp.zeros_like(group))
    hits = (group[:, :, None] == jnp.arange(2 * NZ)[None, None, :]).astype(jnp.int32)
    counts = jnp.sum(hits, axis=1)
    offsets = jnp.cumsum(counts, axis=0) - counts
    number = jnp.sum(counts, axis=0)
    entry = jnp.sum(hits * offsets[:, None, :], axis=2) + rank
    where = jnp.where(match, group * ENTRIES + entry, -1).reshape(-1)
    row = source * NY + block_row // NC
    packed = place + 128 * shift + 512 * (got % BPD) + 16384 * row
    filling = 127
    spots = jnp.arange(2 * NZ * ENTRIES, dtype=jnp.int32)
    table = filling + jnp.sum(
        jnp.where(where[:, None] == spots[None, :], packed.reshape(-1)[:, None] - filling, 0),
        axis=0,
    )

    longest = jnp.max(jnp.where(got >= 0, place, -1)) + 1

    def second_part():
        parts = []
        for dx in range(NX):
            sent = flat_values.at[wanted[dx, FIRST:]].get(mode="promise_in_bounds")
            parts.append(lax.ppermute(sent, "x", ring(NX, dx)) if dx else sent)
        return tuple(parts)

    def no_second_part():
        return (jnp.zeros((REST, BS, BS), jnp.bfloat16),) * NX

    more = lax.cond(longest > FIRST, second_part, no_second_part)
    number = jnp.concatenate([number, longest[None]])

    prev = None
    groups = [((0, 1, 7, 2, 6), FULL), ((3, 5), 3 * CAP), ((4,), CAP)]
    for ds, window in groups:
        prev = products(ds, window, table, number, vals, more, [have[d] for d in ds], prev)
    mine, other = prev
    half = mine + lax.ppermute(other, "core", ring(NC, 1))
    image = jnp.sum(lax.all_to_all(half, ("x", "y"), 0, 0, tiled=True), axis=0)

    gram = lax.dot_general(
        image, image, (((0,), (0,)), ((), ())), precision=HIGH, preferred_element_type=jnp.float32
    )
    plane = ("x", "y", "core")
    n_plane = NX * NY * NC
    piece = K // n_plane
    gram = gram.reshape(n_plane, piece, K)
    part = jnp.sum(lax.all_to_all(gram, plane, 0, 0, tiled=True), axis=0)
    part = jnp.broadcast_to(part[None], (NZ, piece, K))
    part = jnp.sum(lax.all_to_all(part, "z", 0, 0, tiled=True), axis=0) / (NZ * n_plane * BS)
    part = jnp.broadcast_to(part[None], (n_plane, piece, K))
    gram = lax.all_to_all(part, plane, 0, 0, tiled=True).reshape(K, K)
    triangle, basis = factor(gram, image.T)
    return basis, triangle


def solution(mesh):
    axes = ("z", "x", "y", "core")
    fine = Mesh(mesh.devices.reshape(NZ, NX, NY, NC), axes)
    rows, cols = ("z", "x"), ("y", "core")
    return jax.shard_map(
        one_device,
        mesh=fine,
        in_specs=(P(rows, cols, None, None), P(rows, cols), P(rows, cols), P(axes, None)),
        out_specs=(P(axes, None), P()),
        check_vma=False,
    )
```

profile of v0, /device:TPU:2, one launch (start us, length us, event | category | flops | bytes accessed | tf_op | source)
XLA Modules:
  0.0 291.9 jit_solution(3588601704721787226)
XLA Ops:
  3.0 2.8 collective-permute-start.4
  10.7 4.0 %collective-permute-start.13 = (bf16[16,128,256]{2,1,0:T(8,128)(2,1)}, bf16[16,128,256]{2,1,0:T(8,128)(2,1)}, u32[]{:S(2)}, u32[]{:S(2)}) collective-permute-start(bf16[16,128,256]{2,1,0:T(8,128)(2,1)} %get-tuple-element.39), channel_id=1, source_target_pairs={{0,224},{32,0},{64,32},{96,64},{128,96},{160,128},{192,160},{224,1... | collective-permute-start | bytes 3145736 | tf_op jit(solution)/shard_map/ppermute | solution.py:355
  20.2 3.5 %conditional.1 = (bf16[24,128,128]{2,1,0:T(8,128)(2,1)S(1)}, bf16[24,128,128]{2,1,0:T(8,128)(2,1)}, bf16[24,128,128]{2,1,0:T(8,128)(2,1)}, bf16[24,128,128]{2,1,0:T(8,128)(2,1)}) conditional(s32[]{:T(128)} %convert_element_type.19, () %tuple.18, (s32[4,96]{1,0:T(4,128)S(1)}, bf16[256,128,128]{2,1,0:T(8,128)(2,1)}) %tuple.35), branch_computations={%region_10.11_spmd, %region_11.12_spmd} | conditional | flops 4384 | bytes 15746712 | solution.py:431
  25.7 13.1 %collective-permute-done.9.refs_13_ = bf16[16,128,256]{2,1,0:T(8,128)(2,1)S(1)} collective-permute-done((bf16[16,128,256]{2,1,0:T(8,128)(2,1)}, bf16[16,128,256]{2,1,0:T(8,128)(2,1)S(1)}, u32[]{:S(2)}, u32[]{:S(2)}) %collective-permute-start.9) | collective-permute-done | bytes 1048608 | tf_op jit(solution)/shard_map/ppermute | solution.py:354
  38.8 3.4 %collective-permute-start.14 = (bf16[16,128,256]{2,1,0:T(8,128)(2,1)}, bf16[16,128,256]{2,1,0:T(8,128)(2,1)}, u32[]{:S(2)}, u32[]{:S(2)}) collective-permute-start(bf16[16,128,256]{2,1,0:T(8,128)(2,1)} %collective-permute-done.13.refs_12_), channel_id=1, source_target_pairs={{0,224},{32,0},{64,32},{96,64},{128,96},{160,128},{192,160},{224,1... | collective-permute-start | bytes 3145736 | tf_op jit(solution)/shard_map/ppermute | solution.py:385
  42.3 9.6 %shard_map.60 = (bf16[72,128,128]{2,1,0:T(8,128)(2,1)}, bf16[72,128,128]{2,1,0:T(8,128)(2,1)}, bf16[72,128,128]{2,1,0:T(8,128)(2,1)}) custom-call(s32[216]{0:T(256)S(1)} %reshape.1274.index, bf16[256,128,128]{2,1,0:T(8,128)(2,1)} %bitcast.51), custom_call_target="tpu_custom_call" | custom-call | bytes 14155776 | tf_op jit(solution)/shard_map/pallas_call | solution.py:87
  52.1 9.0 %collective-permute-done.17.refs_11_ = bf16[16,128,256]{2,1,0:T(8,128)(2,1)} collective-permute-done((bf16[16,128,256]{2,1,0:T(8,128)(2,1)}, bf16[16,128,256]{2,1,0:T(8,128)(2,1)}, u32[]{:S(2)}, u32[]{:S(2)}) %collective-permute-start.17) | collective-permute-done | bytes 1048608 | tf_op jit(solution)/shard_map/ppermute | solution.py:355
  61.4 3.6 %collective-permute-start.18 = (bf16[16,128,256]{2,1,0:T(8,128)(2,1)}, bf16[16,128,256]{2,1,0:T(8,128)(2,1)}, u32[]{:S(2)}, u32[]{:S(2)}) collective-permute-start(bf16[16,128,256]{2,1,0:T(8,128)(2,1)} %collective-permute-done.17.refs_11_), channel_id=1, source_target_pairs={{0,224},{32,0},{64,32},{96,64},{128,96},{160,128},{192,160},{224,1... | collective-permute-start | bytes 3145736 | tf_op jit(solution)/shard_map/ppermute | solution.py:385
  65.0 17.2 %collective-permute-done.10.refs_17_ = bf16[16,128,256]{2,1,0:T(8,128)(2,1)} collective-permute-done((bf16[16,128,256]{2,1,0:T(8,128)(2,1)S(1)}, bf16[16,128,256]{2,1,0:T(8,128)(2,1)}, u32[]{:S(2)}, u32[]{:S(2)}) %collective-permute-start.10) | collective-permute-done | bytes 1048608 | tf_op jit(solution)/shard_map/ppermute | solution.py:383
  84.9 19.1 %collective-permute-done.18.refs_15_ = bf16[16,128,256]{2,1,0:T(8,128)(2,1)} collective-permute-done((bf16[16,128,256]{2,1,0:T(8,128)(2,1)}, bf16[16,128,256]{2,1,0:T(8,128)(2,1)}, u32[]{:S(2)}, u32[]{:S(2)}) %collective-permute-start.18) | collective-permute-done | bytes 1048608 | tf_op jit(solution)/shard_map/ppermute | solution.py:385
  104.3 3.1 %collective-permute-done.21.refs_18_ = bf16[16,128,256]{2,1,0:T(8,128)(2,1)} collective-permute-done((bf16[16,128,256]{2,1,0:T(8,128)(2,1)}, bf16[16,128,256]{2,1,0:T(8,128)(2,1)}, u32[]{:S(2)}, u32[]{:S(2)}) %collective-permute-start.21) | collective-permute-done | bytes 1048608 | tf_op jit(solution)/shard_map/ppermute | solution.py:383
  110.3 6.7 %collective-permute-done.7.refs_4_ = bf16[72,128,128]{2,1,0:T(8,128)(2,1)} collective-permute-done((bf16[72,128,128]{2,1,0:T(8,128)(2,1)}, bf16[72,128,128]{2,1,0:T(8,128)(2,1)}, u32[]{:S(2)}, u32[]{:S(2)}) %collective-permute-start.7) | collective-permute-done | bytes 2359328 | tf_op jit(solution)/shard_map/ppermute | solution.py:375
  117.4 14.6 %collective-permute-done.11.refs_8_ = bf16[16,128,256]{2,1,0:T(8,128)(2,1)} collective-permute-done((bf16[16,128,256]{2,1,0:T(8,128)(2,1)}, bf16[16,128,256]{2,1,0:T(8,128)(2,1)}, u32[]{:S(2)}, u32[]{:S(2)}) %collective-permute-start.11) | collective-permute-done | bytes 1048608 | tf_op jit(solution)/shard_map/ppermute | solution.py:383
  135.3 3.2 %shard_map.59.refs_2_ = bf16[72,128,128]{2,1,0:T(8,128)(2,1)S(1)} custom-call(s32[72]{0:T(128)S(1)} %slice_bitcast_fusion.index, bf16[256,128,128]{2,1,0:T(8,128)(2,1)} %bitcast.52), custom_call_target="tpu_custom_call" | custom-call | bytes 4718592 | tf_op jit(solution)/shard_map/pallas_call | solution.py:87
  140.8 22.0 %collective-permute-done.8.refs_5_ = bf16[72,128,128]{2,1,0:T(8,128)(2,1)} collective-permute-done((bf16[72,128,128]{2,1,0:T(8,128)(2,1)}, bf16[72,128,128]{2,1,0:T(8,128)(2,1)}, u32[]{:S(2)}, u32[]{:S(2)}) %collective-permute-start.8) | collective-permute-done | bytes 2359328 | tf_op jit(solution)/shard_map/ppermute | solution.py:375
  162.7 13.7 %shard_map.61 = (f32[16,128,256]{2,1,0:T(8,128)S(1)}, f32[16,128,256]{2,1,0:T(8,128)S(1)}) custom-call(s32[768]{0:T(1024)S(1)} %broadcast_add_fusion.refs_0_, s32[17]{0:T(128)S(1)} %pad_add_fusion.1.refs_1_, bf16[72,128,128]{2,1,0:T(8,128)(2,1)} %copy-done, bf16[72,128,128]{2,1,0:T(8,128)(2,1)} %copy-done.2, ...), custom_call_target="tpu_custom_call" | custom-call | flops 838860800 | bytes 23068672 | tf_op jit(solution)/shard_map/pallas_call | solution.py:196
  178.6 5.3 %shard_map.62 = (f32[16,128,256]{2,1,0:T(8,128)S(1)}, f32[16,128,256]{2,1,0:T(8,128)S(1)}) custom-call(s32[768]{0:T(1024)S(1)} %broadcast_add_fusion.refs_0_, s32[17]{0:T(128)S(1)} %pad_add_fusion.1.refs_1_, bf16[72,128,128]{2,1,0:T(8,128)(2,1)S(1)} %copy-done.1, ...), custom_call_target="tpu_custom_call", output_to_operand_aliasing={{0}: (10, {}), {1}: (11, {})} | custom-call | flops 335544320 | bytes 8912896 | tf_op jit(solution)/shard_map/pallas_call | solution.py:196
  186.2 3.4 %shard_map.63 = (f32[16,128,256]{2,1,0:T(8,128)S(1)}, f32[16,128,256]{2,1,0:T(8,128)S(1)}) custom-call(s32[768]{0:T(1024)S(1)} %broadcast_add_fusion.refs_0_, s32[17]{0:T(128)S(1)} %pad_add_fusion.1.refs_1_, bf16[72,128,128]{2,1,0:T(8,128)(2,1)S(1)} %copy-done.1, bf16[72,128,128]{2,1,0:T(8,128)(2,1)S(1)} %copy-done.3, ...), custom_call_target="tpu_custom_call", output_to_operand_aliasing={{0}: (8, {}), {1}: (9, {})} | custom-call | flops 167772160 | bytes 3670016 | tf_op jit(solution)/shard_map/pallas_call | solution.py:196
  189.7 4.1 %collective-permute-done.23 = f32[16,128,256]{2,1,0:T(8,128)S(1)} collective-permute-done((f32[16,128,256]{2,1,0:T(8,128)S(1)}, f32[16,128,256]{2,1,0:T(8,128)S(1)}, u32[]{:S(2)}, u32[]{:S(2)}) %collective-permute-start.23) | collective-permute-done | bytes 2097184 | tf_op jit(solution)/shard_map/ppermute | solution.py:439
  194.1 46.3 %all_to_all.20 = f32[16,128,256]{2,1,0:T(8,128)S(1)} all-to-all(f32[16,128,256]{2,1,0:T(8,128)S(1)} %add.453), channel_id=1, replica_groups=mesh['z'=8,'x'=4,'y'=4,'core'=2] {'x','y'}, dimensions={0} | all-to-all | bytes 4194304 | tf_op jit(solution)/shard_map/all_to_all | solution.py:440
  241.0 13.4 %all_to_all.21 = f32[32,8,256]{2,1,0:T(8,128)S(1)} all-to-all(f32[32,8,256]{2,1,0:T(8,128)S(1)} %fusion.5), channel_id=1, replica_groups=mesh['z'=8,'x'=4,'y'=4,'core'=2] {'x','y','core'}, dimensions={0} | all-to-all | bytes 524288 | tf_op jit(solution)/shard_map/all_to_all | solution.py:449
  254.5 13.3 %all_to_all.22 = f32[8,8,256]{2,1,0:T(8,128)S(1)} all-to-all(f32[8,8,256]{2,1,0:T(8,128)S(1)} %broadcast_in_dim.106), channel_id=1, replica_groups=mesh['z'=8,'x'=4,'y'=4,'core'=2] {'z'}, dimensions={0} | all-to-all | bytes 131072 | tf_op jit(solution)/shard_map/all_to_all | solution.py:451
  267.8 12.6 %all_to_all.23 = f32[32,8,256]{2,1,0:T(8,128)} all-to-all(f32[32,8,256]{2,1,0:T(8,128)S(1)} %broadcast_in_dim.107), channel_id=1, replica_groups=mesh['z'=8,'x'=4,'y'=4,'core'=2] {'x','y','core'}, dimensions={0} | all-to-all | bytes 524288 | tf_op jit(solution)/shard_map/all_to_all | solution.py:453
  280.4 11.5 %factor.1 = (f32[256,256]{1,0:T(8,128)}, f32[128,256]{1,0:T(8,128)}) custom-call(f32[256,256]{1,0:T(8,128)} %bitcast.56, f32[256,128]{1,0:T(8,128)} %bitcast.55), custom_call_target="tpu_custom_call" | custom-call | tf_op jit(solution)/shard_map/factor/pallas_call | solution.py:310
  (103 shorter events, 35.2 us)
Async XLA Ops:
  1.5 13.8 %collective-permute-start.3 = (s32[2,128]{1,0:T(2,128)S(1)}, s32[2,128]{1,0:T(2,128)S(1)}, u32[]{:S(2)}, u32[]{:S(2)}) collective-permute-start(s32[2,128]{1,0:T(2,128)S(1)} %reshape_reshape.3.x_ref), channel_id=1, source_target_pairs={{0,8},{8,16},{16,24},{24,0},{1,9},{9,17},{17,25},{25,1},{2,10},{10... | collective-permute-start | bytes 3080 | tf_op jit(solution)/shard_map/ppermute | solution.py:371
  3.0 12.3 %collective-permute-start.4 = (s32[2,128]{1,0:T(2,128)S(1)}, s32[2,128]{1,0:T(2,128)S(1)}, u32[]{:S(2)}, u32[]{:S(2)}) collective-permute-start(s32[2,128]{1,0:T(2,128)S(1)} %reshape_reshape.3.x_ref), channel_id=1, source_target_pairs={{0,16},{8,24},{16,0},{24,8},{1,17},{9,25},{17,1},{25,9},{2,18},{10... | collective-permute-start | bytes 3080 | tf_op jit(solution)/shard_map/ppermute | solution.py:371
  5.8 9.5 %collective-permute-start.5 = (s32[2,128]{1,0:T(2,128)S(1)}, s32[2,128]{1,0:T(2,128)S(1)}, u32[]{:S(2)}, u32[]{:S(2)}) collective-permute-start(s32[2,128]{1,0:T(2,128)S(1)} %reshape_reshape.3.x_ref), channel_id=1, source_target_pairs={{0,24},{8,0},{16,8},{24,16},{1,25},{9,1},{17,9},{25,17},{2,26},{10... | collective-permute-start | bytes 3080 | tf_op jit(solution)/shard_map/ppermute | solution.py:371
  8.7 30.2 %collective-permute-start.9 = (bf16[16,128,256]{2,1,0:T(8,128)(2,1)}, bf16[16,128,256]{2,1,0:T(8,128)(2,1)S(1)}, u32[]{:S(2)}, u32[]{:S(2)}) collective-permute-start(bf16[16,128,256]{2,1,0:T(8,128)(2,1)} %get-tuple-element.38), channel_id=1, source_target_pairs={{0,32},{32,64},{64,96},{96,128},{128,160},{160,192},{192,224},{224... | collective-permute-start | bytes 3145736 | tf_op jit(solution)/shard_map/ppermute | solution.py:354
  10.7 28.2 %collective-permute-start.13 = (bf16[16,128,256]{2,1,0:T(8,128)(2,1)}, bf16[16,128,256]{2,1,0:T(8,128)(2,1)}, u32[]{:S(2)}, u32[]{:S(2)}) collective-permute-start(bf16[16,128,256]{2,1,0:T(8,128)(2,1)} %get-tuple-element.39), channel_id=1, source_target_pairs={{0,224},{32,0},{64,32},{96,64},{128,96},{160,128},{192,160},{224,1... | collective-permute-start | bytes 3145736 | tf_op jit(solution)/shard_map/ppermute | solution.py:355
  23.7 37.3 %collective-permute-start.17 = (bf16[16,128,256]{2,1,0:T(8,128)(2,1)}, bf16[16,128,256]{2,1,0:T(8,128)(2,1)}, u32[]{:S(2)}, u32[]{:S(2)}) collective-permute-start(bf16[16,128,256]{2,1,0:T(8,128)(2,1)} %get-tuple-element.38), channel_id=1, source_target_pairs={{0,224},{32,0},{64,32},{96,64},{128,96},{160,128},{192,160},{224,1... | collective-permute-start | bytes 3145736 | tf_op jit(solution)/shard_map/ppermute | solution.py:355
  25.6 35.8 %collective-permute-start.20 = (bf16[16,128,256]{2,1,0:T(8,128)(2,1)}, bf16[16,128,256]{2,1,0:T(8,128)(2,1)}, u32[]{:S(2)}, u32[]{:S(2)}) collective-permute-start(bf16[16,128,256]{2,1,0:T(8,128)(2,1)} %get-tuple-element.39), channel_id=1, source_target_pairs={{0,32},{32,64},{64,96},{96,128},{128,160},{160,192},{192,224},{224... | collective-permute-start | bytes 3145736 | tf_op jit(solution)/shard_map/ppermute | solution.py:354
  38.8 43.4 %collective-permute-start.10 = (bf16[16,128,256]{2,1,0:T(8,128)(2,1)S(1)}, bf16[16,128,256]{2,1,0:T(8,128)(2,1)}, u32[]{:S(2)}, u32[]{:S(2)}) collective-permute-start(bf16[16,128,256]{2,1,0:T(8,128)(2,1)S(1)} %collective-permute-done.9.refs_13_), channel_id=1, source_target_pairs={{0,32},{32,64},{64,96},{96,128},{128,160},{160,192},{192,224},{224... | collective-permute-start | bytes 3145736 | tf_op jit(solution)/shard_map/ppermute | solution.py:383
  38.8 44.7 %collective-permute-start.14 = (bf16[16,128,256]{2,1,0:T(8,128)(2,1)}, bf16[16,128,256]{2,1,0:T(8,128)(2,1)}, u32[]{:S(2)}, u32[]{:S(2)}) collective-permute-start(bf16[16,128,256]{2,1,0:T(8,128)(2,1)} %collective-permute-done.13.refs_12_), channel_id=1, source_target_pairs={{0,224},{32,0},{64,32},{96,64},{128,96},{160,128},{192,160},{224,1... | collective-permute-start | bytes 3145736 | tf_op jit(solution)/shard_map/ppermute | solution.py:385
  52.0 56.2 %collective-permute-start.6 = (bf16[72,128,128]{2,1,0:T(8,128)(2,1)}, bf16[72,128,128]{2,1,0:T(8,128)(2,1)S(1)}, u32[]{:S(2)}, u32[]{:S(2)}) collective-permute-start(bf16[72,128,128]{2,1,0:T(8,128)(2,1)} %get-tuple-element.35), channel_id=1, source_target_pairs={{0,8},{8,16},{16,24},{24,0},{1,9},{9,17},{17,25},{25,1},{2,10},{10... | collective-permute-start | bytes 7077896 | tf_op jit(solution)/shard_map/ppermute | solution.py:375
  61.0 56.0 %collective-permute-start.7 = (bf16[72,128,128]{2,1,0:T(8,128)(2,1)}, bf16[72,128,128]{2,1,0:T(8,128)(2,1)}, u32[]{:S(2)}, u32[]{:S(2)}) collective-permute-start(bf16[72,128,128]{2,1,0:T(8,128)(2,1)} %get-tuple-element.36), channel_id=1, source_target_pairs={{0,16},{8,24},{16,0},{24,8},{1,17},{9,25},{17,1},{25,9},{2,18},{10... | collective-permute-start | bytes 7077896 | tf_op jit(solution)/shard_map/ppermute | solution.py:375
  61.4 42.6 %collective-permute-start.18 = (bf16[16,128,256]{2,1,0:T(8,128)(2,1)}, bf16[16,128,256]{2,1,0:T(8,128)(2,1)}, u32[]{:S(2)}, u32[]{:S(2)}) collective-permute-start(bf16[16,128,256]{2,1,0:T(8,128)(2,1)} %collective-permute-done.17.refs_11_), channel_id=1, source_target_pairs={{0,224},{32,0},{64,32},{96,64},{128,96},{160,128},{192,160},{224,1... | collective-permute-start | bytes 3145736 | tf_op jit(solution)/shard_map/ppermute | solution.py:385
  82.2 25.2 %collective-permute-start.21 = (bf16[16,128,256]{2,1,0:T(8,128)(2,1)}, bf16[16,128,256]{2,1,0:T(8,128)(2,1)}, u32[]{:S(2)}, u32[]{:S(2)}) collective-permute-start(bf16[16,128,256]{2,1,0:T(8,128)(2,1)} %collective-permute-done.20.refs_14_), channel_id=1, source_target_pairs={{0,32},{32,64},{64,96},{96,128},{128,160},{160,192},{192,224},{224... | collective-permute-start | bytes 3145736 | tf_op jit(solution)/shard_map/ppermute | solution.py:383
  83.5 79.2 %collective-permute-start.8 = (bf16[72,128,128]{2,1,0:T(8,128)(2,1)}, bf16[72,128,128]{2,1,0:T(8,128)(2,1)}, u32[]{:S(2)}, u32[]{:S(2)}) collective-permute-start(bf16[72,128,128]{2,1,0:T(8,128)(2,1)} %get-tuple-element.37), channel_id=1, source_target_pairs={{0,24},{8,0},{16,8},{24,16},{1,25},{9,1},{17,9},{25,17},{2,26},{10... | collective-permute-start | bytes 7077896 | tf_op jit(solution)/shard_map/ppermute | solution.py:375
  104.0 28.0 %collective-permute-start.11 = (bf16[16,128,256]{2,1,0:T(8,128)(2,1)}, bf16[16,128,256]{2,1,0:T(8,128)(2,1)}, u32[]{:S(2)}, u32[]{:S(2)}) collective-permute-start(bf16[16,128,256]{2,1,0:T(8,128)(2,1)} %collective-permute-done.10.refs_17_), channel_id=1, source_target_pairs={{0,32},{32,64},{64,96},{96,128},{128,160},{160,192},{192,224},{224... | collective-permute-start | bytes 3145736 | tf_op jit(solution)/shard_map/ppermute | solution.py:383
  107.4 26.3 %collective-permute-start.15 = (bf16[16,128,256]{2,1,0:T(8,128)(2,1)}, bf16[16,128,256]{2,1,0:T(8,128)(2,1)}, u32[]{:S(2)}, u32[]{:S(2)}) collective-permute-start(bf16[16,128,256]{2,1,0:T(8,128)(2,1)} %collective-permute-done.14.refs_16_), channel_id=1, source_target_pairs={{0,224},{32,0},{64,32},{96,64},{128,96},{160,128},{192,160},{224,1... | collective-permute-start | bytes 3145736 | tf_op jit(solution)/shard_map/ppermute | solution.py:385
  108.2 30.3 %copy-start.2 = (bf16[72,128,128]{2,1,0:T(8,128)(2,1)}, bf16[72,128,128]{2,1,0:T(8,128)(2,1)S(1)}, u32[]{:S(2)}) copy-start(bf16[72,128,128]{2,1,0:T(8,128)(2,1)S(1)} %collective-permute-done.6.refs_3_) | copy-start | bytes 7077892
  108.2 68.2 %collective-permute-start.19 = (bf16[16,128,256]{2,1,0:T(8,128)(2,1)}, bf16[16,128,256]{2,1,0:T(8,128)(2,1)S(1)}, u32[]{:S(2)}, u32[]{:S(2)}) collective-permute-start(bf16[16,128,256]{2,1,0:T(8,128)(2,1)} %collective-permute-done.18.refs_15_), channel_id=1, source_target_pairs={{0,224},{32,0},{64,32},{96,64},{128,96},{160,128},{192,160},{224,1... | collective-permute-start | bytes 3145736 | tf_op jit(solution)/shard_map/ppermute | solution.py:385
  117.0 60.4 %collective-permute-start.22 = (bf16[16,128,256]{2,1,0:T(8,128)(2,1)}, bf16[16,128,256]{2,1,0:T(8,128)(2,1)S(1)}, u32[]{:S(2)}, u32[]{:S(2)}) collective-permute-start(bf16[16,128,256]{2,1,0:T(8,128)(2,1)} %collective-permute-done.21.refs_18_), channel_id=1, source_target_pairs={{0,32},{32,64},{64,96},{96,128},{128,160},{160,192},{192,224},{224... | collective-permute-start | bytes 3145736 | tf_op jit(solution)/shard_map/ppermute | solution.py:383
  132.0 51.9 %collective-permute-start.12 = (bf16[16,128,256]{2,1,0:T(8,128)(2,1)}, bf16[16,128,256]{2,1,0:T(8,128)(2,1)S(1)}, u32[]{:S(2)}, u32[]{:S(2)}) collective-permute-start(bf16[16,128,256]{2,1,0:T(8,128)(2,1)} %collective-permute-done.11.refs_8_), channel_id=1, source_target_pairs={{0,32},{32,64},{64,96},{96,128},{128,160},{160,192},{192,224},{224... | collective-permute-start | bytes 3145736 | tf_op jit(solution)/shard_map/ppermute | solution.py:383
  133.7 51.2 %collective-permute-start.16 = (bf16[16,128,256]{2,1,0:T(8,128)(2,1)}, bf16[16,128,256]{2,1,0:T(8,128)(2,1)}, u32[]{:S(2)}, u32[]{:S(2)}) collective-permute-start(bf16[16,128,256]{2,1,0:T(8,128)(2,1)} %collective-permute-done.15.refs_7_), channel_id=1, source_target_pairs={{0,224},{32,0},{64,32},{96,64},{128,96},{160,128},{192,160},{224,1... | collective-permute-start | bytes 3145736 | tf_op jit(solution)/shard_map/ppermute | solution.py:385
  135.3 27.5 %copy-start.9 = (bf16[24,128,128]{2,1,0:T(8,128)(2,1)S(1)}, bf16[24,128,128]{2,1,0:T(8,128)(2,1)}, u32[]{:S(2)}) copy-start(bf16[24,128,128]{2,1,0:T(8,128)(2,1)} %copy-done.8) | copy-start | bytes 2359300
  189.6 4.2 %collective-permute-start.23 = (f32[16,128,256]{2,1,0:T(8,128)S(1)}, f32[16,128,256]{2,1,0:T(8,128)S(1)}, u32[]{:S(2)}, u32[]{:S(2)}) collective-permute-start(f32[16,128,256]{2,1,0:T(8,128)S(1)} %get-tuple-element.49), channel_id=1, source_target_pairs={{0,1},{1,0},{2,3},{3,2},{4,5},{5,4},{6,7},{7,6},{8,9},{9,8},{10,11... | collective-permute-start | bytes 6291464 | tf_op jit(solution)/shard_map/ppermute | solution.py:439
  240.6 39.7 %copy-start.10 = (f32[128,256]{0,1:T(8,128)}, f32[128,256]{0,1:T(8,128)S(1)}, u32[]{:S(2)}) copy-start(f32[128,256]{0,1:T(8,128)S(1)} %copy.12) | copy-start | bytes 393220
  (9 other events, 67.6 us)
where the time goes:
time: 295 us; the launch traced here: 292 us
  waiting for transfers between devices  112 us (38%)
  blocking collectives  85.5 us (29%)
  Pallas kernels  50.4 us (17%)
  starting transfers between devices  26.3 us (9%)
  local copies, waits for them, and re-layouts  9.79 us (3%)
  other arithmetic  5.83 us (2%)
    all_to_all x1, blocking collectives, one_device(): image = jnp.sum(lax.all_to_all(half, ('x', 'y'), 0, 0, tiled=True), axis=0)  46.3 us
    ppermute x5, waiting for transfers between devices, one_device(): fwd[step][h] = lax.ppermute(fwd[step - 1][h], 'z', ring(NZ, 1))  34.9 us
    ppermute x3, waiting for transfers between devices, one_device(): vals[dx] = lax.ppermute(vals[dx], 'x', ring(NX, dx))  28.7 us
    pallas_call x3, Pallas kernels, products(): pl.pallas_call(functools.partial(products_kernel, ds, halves, window, fir...  22.4 us
    ppermute x5, waiting for transfers between devices, one_device(): bwd[step][h] = lax.ppermute(bwd[step - 1][h], 'z', ring(NZ, -1))  22.1 us
    all_to_all x1, blocking collectives, one_device(): part = jnp.sum(lax.all_to_all(gram, plane, 0, 0, tiled=True), axis=0)  13.4 us
    all_to_all x1, blocking collectives, one_device(): lax.all_to_all(part, 'z', 0, 0, tiled=True)  13.3 us
    ppermute x2, waiting for transfers between devices, one_device(): fwd = {1: [lax.ppermute(blocks[h], 'z', ring(NZ, 1)) for h in range(2)]}  13.2 us
  transfers between devices with their start and end apart: 21, of which 12 were waited for; matrix products, arithmetic and copies ran while one was open for 3% of the time, Pallas kernels for 12%

commit v1 on v0

--- a/solution.py
+++ b/solution.py
@@ -216,6 +216,77 @@
 
 
 HB = 64
+
+
+def spread_kernel(mine, theirs, *outs):
+    top, bottom = outs[:NX], outs[NX:]
+    half = BS // 2
+    for r in range(NX):
+
+        def step(j, carry, r=r):
+            i = NY * r + j
+            top[r][j] = mine[i, :half] + theirs[i, :half]
+            i = NY * j + r
+            bottom[r][j] = mine[i, half:] + theirs[i, half:]
+            return carry
+
+        lax.fori_loop(0, NX, step, 0)
+
+
+def add_up_kernel(*refs):
+    outs = refs[2 * NX :]
+    for side in range(2):
+        ins = refs[side * NX : (side + 1) * NX]
+        for r in range(NX):
+            outs[side * NX + r][...] = (ins[0][r] + ins[1][r]) + (ins[2][r] + ins[3][r])
+
+
+def in_vmem(kernel, args, shape):
+    vm = pl.BlockSpec(memory_space=pltpu.VMEM)
+    out = pl.pallas_call(
+        kernel,
+        out_shape=[jax.ShapeDtypeStruct(shape, jnp.float32)] * (2 * NX),
+        in_specs=[vm] * len(args),
+        out_specs=[vm] * (2 * NX),
+        compiler_params=pltpu.CompilerParams(vmem_limit_bytes=16 << 20),
+    )(*args)
+    return out[:NX], out[NX:]
+
+
+def local_gram_kernel(*refs):
+    gram, image_t = refs[2 * NX :]
+    sides = [
+        (side[0][...] + side[1][...]) + (side[2][...] + side[3][...])
+        for side in (refs[:NX], refs[NX : 2 * NX])
+    ]
+    image = jnp.concatenate(sides, axis=0)
+    image_t[...] = image.T
+    gram[...] = lax.dot_general(
+        image, image, (((0,), (0,)), ((), ())), precision=HIGH, preferred_element_type=jnp.float32
+    )
+
+
+def local_gram(top, bottom):
+    vm = pl.BlockSpec(memory_space=pltpu.VMEM)
+    return pl.pallas_call(
+        local_gram_kernel,
+        out_shape=[
+            jax.ShapeDtypeStruct((K, K), jnp.float32),
+            jax.ShapeDtypeStruct((K, BS), jnp.float32),
+        ],
+        in_specs=[vm] * (2 * NX),
+        out_specs=[vm, vm],
+        compiler_params=pltpu.CompilerParams(vmem_limit_bytes=16 << 20),
+        name="local_gram",
+    )(*top, *bottom)
+
+
+def spread(mine, theirs):
+    return in_vmem(spread_kernel, (mine, theirs), (NY, BS // 2, K))
+
+
+def add_up(top, bottom):
+    return in_vmem(add_up_kernel, (*top, *bottom), (BS // 2, K))
 
 
 def factor_block(d):
@@ -268,40 +339,40 @@
     low = lane < HB
     rown = lax.broadcasted_iota(jnp.int32, (HB, K), 0)
     coln = lax.broadcasted_iota(jnp.int32, (HB, K), 1)
-    for b in range(K // HB):
-        lo, hi = b * HB, (b + 1) * HB
-        tile = a_ref[lo:hi, 128 * (b // 2) : 128 * (b // 2) + 128]
-        if b % 2:
-            tile = pltpu.roll(tile, HB, 1)
+
+    def one_block(b, carry):
+        lo = pl.multiple_of(b * HB, HB)
+        here = a_ref[pl.ds(lo, HB), :]
+        tile = jnp.where(b >= 2, here[:, 128:], here[:, :128])
+        tile = jnp.where(b % 2 == 1, pltpu.roll(tile, HB, 1), tile)
         res = factor_block(jnp.where(low, tile, eye))
         inv = jnp.where(low, 0.0, res)
-        left = lo // 128 * 128
-        zero = jnp.zeros((HB, K - left + BS), jnp.float32)
-        both = jnp.concatenate([a_ref[lo:hi, left:], w_ref[lo:hi, :]], axis=1)
+        both = jnp.concatenate([here, w_ref[pl.ds(lo, HB), :]], axis=1)
         out = jnp.dot(
             inv,
-            jnp.concatenate([zero, both], axis=0),
+            jnp.concatenate([jnp.zeros_like(both), both], axis=0),
             precision=HIGH,
             preferred_element_type=jnp.float32,
         )
-        upper = jnp.where((coln >= rown + lo)[:, left:], out[:, : K - left], 0.0)
-        if left:
-            tri_ref[lo:hi, :left] = jnp.zeros((HB, left), jnp.float32)
-        tri_ref[lo:hi, left:] = upper
-        w_ref[lo:hi, :] = out[:, K - left :]
-        if hi < K:
-            rest = hi // 128 * 128
-            part = upper[:, rest - left :]
-            new = jnp.concatenate([part, out[:, K - left :]], axis=1)
+        upper = jnp.where(coln >= rown + lo, out[:, :K], 0.0)
+        tri_ref[pl.ds(lo, HB), :] = upper
+        w_ref[pl.ds(lo, HB), :] = out[:, K:]
+
+        @pl.when(b < K // HB - 1)
+        def _():
             upd = lax.dot_general(
-                part,
-                new,
+                jnp.where(coln >= lo + HB, upper, 0.0),
+                jnp.concatenate([upper, out[:, K:]], axis=1),
                 (((0,), (0,)), ((), ())),
                 precision=HIGH,
                 preferred_element_type=jnp.float32,
             )
-            a_ref[hi:, rest:] = a_ref[hi:, rest:] - upd[hi - rest :, : K - rest]
-            w_ref[hi:, :] = w_ref[hi:, :] - upd[hi - rest :, K - rest :]
+            a_ref[...] = a_ref[...] - upd[:, :K]
+            w_ref[...] = w_ref[...] - upd[:, K:]
+
+        return carry
+
+    lax.fori_loop(0, K // HB, one_block, 0)
     basis_ref[...] = w_ref[...].T
 
 
@@ -348,7 +419,8 @@
 
 
 def one_device(block_values, block_columns, row_counts, sketch):
-    z, x, core = lax.axis_index("z"), lax.axis_index("x"), lax.axis_index("core")
+    z, x = lax.axis_index("z"), lax.axis_index("x")
+    y, core = lax.axis_index("y"), lax.axis_index("core")
     blocks = split(sketch.reshape(BPD, BS, K))
     have = {0: [sketch.reshape(BPD, BS, K)]}
     fwd = {1: [lax.ppermute(blocks[h], "z", ring(NZ, 1)) for h in range(2)]}
@@ -393,7 +465,6 @@
     got = jnp.stack([m.reshape(slots) for m in metas])
     own = got // BPD
     shift = jnp.arange(NX, dtype=jnp.int32)[:, None]
-    source = (x - shift) % NX
     towards = jnp.where(got < 0, NX, own % NX)
     match = towards == x
     dist = (own // NX - z) % NZ
@@ -407,7 +478,7 @@
     number = jnp.sum(counts, axis=0)
     entry = jnp.sum(hits * offsets[:, None, :], axis=2) + rank
     where = jnp.where(match, group * ENTRIES + entry, -1).reshape(-1)
-    row = source * NY + block_row // NC
+    row = (NX - shift) % NX * NY + (block_row // NC - y) % NY
     packed = place + 128 * shift + 512 * (got % BPD) + 16384 * row
     filling = 127
     spots = jnp.arange(2 * NZ * ENTRIES, dtype=jnp.int32)
@@ -436,12 +507,15 @@
     for ds, window in groups:
         prev = products(ds, window, table, number, vals, more, [have[d] for d in ds], prev)
     mine, other = prev
-    half = mine + lax.ppermute(other, "core", ring(NC, 1))
-    image = jnp.sum(lax.all_to_all(half, ("x", "y"), 0, 0, tiled=True), axis=0)
-
-    gram = lax.dot_general(
-        image, image, (((0,), (0,)), ((), ())), precision=HIGH, preferred_element_type=jnp.float32
-    )
+    parts = spread(mine, lax.ppermute(other, "core", ring(NC, 1)))
+    for axes in (("x", "y"), ("y", "x")):
+        moved = [
+            [part if r == 0 else lax.ppermute(part, axis, ring(NX, r)) for r, part in enumerate(side)]
+            for axis, side in zip(axes, parts)
+        ]
+        if axes[0] == "x":
+            parts = add_up(*moved)
+    gram, image_t = local_gram(*moved)
     plane = ("x", "y", "core")
     n_plane = NX * NY * NC
     piece = K // n_plane
@@ -451,7 +525,7 @@
     part = jnp.sum(lax.all_to_all(part, "z", 0, 0, tiled=True), axis=0) / (NZ * n_plane * BS)
     part = jnp.broadcast_to(part[None], (n_plane, piece, K))
     gram = lax.all_to_all(part, plane, 0, 0, tiled=True).reshape(K, K)
-    triangle, basis = factor(gram, image.T)
+    triangle, basis = factor(gram, image_t)
     return basis, triangle
 
 

time: 295 us -> 298 us (1.010)
  blocking collectives: 85.5 us -> 38.8 us
  starting transfers between devices: 26.3 us -> 65 us
  waiting for transfers between devices: 112 us -> 123 us
    all_to_all x1 -> x0, blocking collectives: 46.3 us -> none  [one_device(): image = jnp.sum(lax.all_to_all(half, ('x', 'y'), 0, 0, tiled=True), axis=0)]
    ppermute x1 -> x13, starting transfers between devices: 0.09 us -> 38.8 us  [the longest x12 38.7 us: one_device(): lax.ppermute(part, axis, ring(NX, r))]
    ppermute x1 -> x13, waiting for transfers between devices: 4.15 us -> 14.6 us  [the longest x12 10.5 us: one_device(): lax.ppermute(part, axis, ring(NX, r))]
  transfers between devices with their start and end apart: 21 -> 33, of which waited for: 12 -> 19; matrix products, arithmetic and copies ran while one was open for 3% -> 3% of each run, Pallas kernels for 12% -> 12%
where the time goes in v1:
time: 298 us; the launch traced here: 295 us
  waiting for transfers between devices  123 us (41%)
  starting transfers between devices  65 us (22%)
  Pallas kernels  51.7 us (17%)
  blocking collectives  38.8 us (13%)
  local copies, waits for them, and re-layouts  10.3 us (3%)
  other arithmetic  5.43 us (2%)
    ppermute x12, starting transfers between devices, one_device(): lax.ppermute(part, axis, ring(NX, r))  38.7 us
    ppermute x5, waiting for transfers between devices, one_device(): fwd[step][h] = lax.ppermute(fwd[step - 1][h], 'z', ring(NZ, 1))  34.9 us
    ppermute x3, waiting for transfers between devices, one_device(): vals[dx] = lax.ppermute(vals[dx], 'x', ring(NX, dx))  28.7 us
    pallas_call x3, Pallas kernels, products(): pl.pallas_call(functools.partial(products_kernel, ds, halves, window, fir...  22.4 us
    ppermute x5, waiting for transfers between devices, one_device(): bwd[step][h] = lax.ppermute(bwd[step - 1][h], 'z', ring(NZ, -1))  22.1 us
    all_to_all x1, blocking collectives, one_device(): lax.all_to_all(part, 'z', 0, 0, tiled=True)  13.4 us
    ppermute x2, waiting for transfers between devices, one_device(): fwd = {1: [lax.ppermute(blocks[h], 'z', ring(NZ, 1)) for h in range(2)]}  13.3 us
    all_to_all x1, blocking collectives, one_device(): part = jnp.sum(lax.all_to_all(gram, plane, 0, 0, tiled=True), axis=0)  12.9 us
  transfers between devices with their start and end apart: 33, of which 19 were waited for; matrix products, arithmetic and copies ran while one was open for 3% of the time, Pallas kernels for 12%

profile of v1, /device:TPU:2, one launch (start us, length us, event | category | flops | bytes accessed | tf_op | source)
XLA Modules:
  0.0 295.5 jit_solution(1195989169082400690)
XLA Ops:
  10.7 4.0 %collective-permute-start.13 = (bf16[16,128,256]{2,1,0:T(8,128)(2,1)}, bf16[16,128,256]{2,1,0:T(8,128)(2,1)}, u32[]{:S(2)}, u32[]{:S(2)}) collective-permute-start(bf16[16,128,256]{2,1,0:T(8,128)(2,1)} %get-tuple-element.57), channel_id=1, source_target_pairs={{0,224},{32,0},{64,32},{96,64},{128,96},{160,128},{192,160},{224,1... | collective-permute-start | bytes 3145736 | tf_op jit(solution)/shard_map/ppermute | solution.py:427
  25.7 13.2 %collective-permute-done.9.refs_13_ = bf16[16,128,256]{2,1,0:T(8,128)(2,1)S(1)} collective-permute-done((bf16[16,128,256]{2,1,0:T(8,128)(2,1)}, bf16[16,128,256]{2,1,0:T(8,128)(2,1)S(1)}, u32[]{:S(2)}, u32[]{:S(2)}) %collective-permute-start.9) | collective-permute-done | bytes 1048608 | tf_op jit(solution)/shard_map/ppermute | solution.py:426
  38.8 3.4 %collective-permute-start.14 = (bf16[16,128,256]{2,1,0:T(8,128)(2,1)}, bf16[16,128,256]{2,1,0:T(8,128)(2,1)}, u32[]{:S(2)}, u32[]{:S(2)}) collective-permute-start(bf16[16,128,256]{2,1,0:T(8,128)(2,1)} %collective-permute-done.13.refs_12_), channel_id=1, source_target_pairs={{0,224},{32,0},{64,32},{96,64},{128,96},{160,128},{192,160},{224,1... | collective-permute-start | bytes 3145736 | tf_op jit(solution)/shard_map/ppermute | solution.py:457
  42.3 9.6 %shard_map.60 = (bf16[72,128,128]{2,1,0:T(8,128)(2,1)}, bf16[72,128,128]{2,1,0:T(8,128)(2,1)}, bf16[72,128,128]{2,1,0:T(8,128)(2,1)}) custom-call(s32[216]{0:T(256)S(1)} %reshape.1294.index, bf16[256,128,128]{2,1,0:T(8,128)(2,1)} %bitcast.45), custom_call_target="tpu_custom_call" | custom-call | bytes 14155776 | tf_op jit(solution)/shard_map/pallas_call | solution.py:87
  52.1 9.0 %collective-permute-done.17.refs_11_ = bf16[16,128,256]{2,1,0:T(8,128)(2,1)} collective-permute-done((bf16[16,128,256]{2,1,0:T(8,128)(2,1)}, bf16[16,128,256]{2,1,0:T(8,128)(2,1)}, u32[]{:S(2)}, u32[]{:S(2)}) %collective-permute-start.17) | collective-permute-done | bytes 1048608 | tf_op jit(solution)/shard_map/ppermute | solution.py:427
  61.4 3.6 %collective-permute-start.18 = (bf16[16,128,256]{2,1,0:T(8,128)(2,1)}, bf16[16,128,256]{2,1,0:T(8,128)(2,1)}, u32[]{:S(2)}, u32[]{:S(2)}) collective-permute-start(bf16[16,128,256]{2,1,0:T(8,128)(2,1)} %collective-permute-done.17.refs_11_), channel_id=1, source_target_pairs={{0,224},{32,0},{64,32},{96,64},{128,96},{160,128},{192,160},{224,1... | collective-permute-start | bytes 3145736 | tf_op jit(solution)/shard_map/ppermute | solution.py:457
  65.0 17.2 %collective-permute-done.10.refs_17_ = bf16[16,128,256]{2,1,0:T(8,128)(2,1)} collective-permute-done((bf16[16,128,256]{2,1,0:T(8,128)(2,1)S(1)}, bf16[16,128,256]{2,1,0:T(8,128)(2,1)}, u32[]{:S(2)}, u32[]{:S(2)}) %collective-permute-start.10) | collective-permute-done | bytes 1048608 | tf_op jit(solution)/shard_map/ppermute | solution.py:455
  84.9 19.1 %collective-permute-done.18.refs_15_ = bf16[16,128,256]{2,1,0:T(8,128)(2,1)} collective-permute-done((bf16[16,128,256]{2,1,0:T(8,128)(2,1)}, bf16[16,128,256]{2,1,0:T(8,128)(2,1)}, u32[]{:S(2)}, u32[]{:S(2)}) %collective-permute-start.18) | collective-permute-done | bytes 1048608 | tf_op jit(solution)/shard_map/ppermute | solution.py:457
  110.3 6.7 %collective-permute-done.7.refs_4_ = bf16[72,128,128]{2,1,0:T(8,128)(2,1)} collective-permute-done((bf16[72,128,128]{2,1,0:T(8,128)(2,1)}, bf16[72,128,128]{2,1,0:T(8,128)(2,1)}, u32[]{:S(2)}, u32[]{:S(2)}) %collective-permute-start.7) | collective-permute-done | bytes 2359328 | tf_op jit(solution)/shard_map/ppermute | solution.py:447
  117.4 14.6 %collective-permute-done.11.refs_8_ = bf16[16,128,256]{2,1,0:T(8,128)(2,1)} collective-permute-done((bf16[16,128,256]{2,1,0:T(8,128)(2,1)}, bf16[16,128,256]{2,1,0:T(8,128)(2,1)}, u32[]{:S(2)}, u32[]{:S(2)}) %collective-permute-start.11) | collective-permute-done | bytes 1048608 | tf_op jit(solution)/shard_map/ppermute | solution.py:455
  140.8 22.0 %collective-permute-done.8.refs_5_ = bf16[72,128,128]{2,1,0:T(8,128)(2,1)} collective-permute-done((bf16[72,128,128]{2,1,0:T(8,128)(2,1)}, bf16[72,128,128]{2,1,0:T(8,128)(2,1)}, u32[]{:S(2)}, u32[]{:S(2)}) %collective-permute-start.8) | collective-permute-done | bytes 2359328 | tf_op jit(solution)/shard_map/ppermute | solution.py:447
  162.7 13.7 %shard_map.61 = (f32[16,128,256]{2,1,0:T(8,128)S(1)}, f32[16,128,256]{2,1,0:T(8,128)S(1)}) custom-call(s32[768]{0:T(1024)S(1)} %broadcast_add_fusion.refs_0_, s32[17]{0:T(128)S(1)} %pad_add_fusion.1.refs_1_, bf16[72,128,128]{2,1,0:T(8,128)(2,1)} %copy-done, bf16[72,128,128]{2,1,0:T(8,128)(2,1)} %copy-done.2, ...), custom_call_target="tpu_custom_call" | custom-call | flops 838860800 | bytes 23068672 | tf_op jit(solution)/shard_map/pallas_call | solution.py:196
  178.7 5.3 %shard_map.62 = (f32[16,128,256]{2,1,0:T(8,128)S(1)}, f32[16,128,256]{2,1,0:T(8,128)S(1)}) custom-call(s32[768]{0:T(1024)S(1)} %broadcast_add_fusion.refs_0_, s32[17]{0:T(128)S(1)} %pad_add_fusion.1.refs_1_, bf16[72,128,128]{2,1,0:T(8,128)(2,1)S(1)} %copy-done.1, ...), custom_call_target="tpu_custom_call", output_to_operand_aliasing={{0}: (10, {}), {1}: (11, {})} | custom-call | flops 335544320 | bytes 8912896 | tf_op jit(solution)/shard_map/pallas_call | solution.py:196
  186.2 3.4 %shard_map.63 = (f32[16,128,256]{2,1,0:T(8,128)S(1)}, f32[16,128,256]{2,1,0:T(8,128)S(1)}) custom-call(s32[768]{0:T(1024)S(1)} %broadcast_add_fusion.refs_0_, s32[17]{0:T(128)S(1)} %pad_add_fusion.1.refs_1_, bf16[72,128,128]{2,1,0:T(8,128)(2,1)S(1)} %copy-done.1, bf16[72,128,128]{2,1,0:T(8,128)(2,1)S(1)} %copy-done.3, ...), custom_call_target="tpu_custom_call", output_to_operand_aliasing={{0}: (8, {}), {1}: (9, {})} | custom-call | flops 167772160 | bytes 3670016 | tf_op jit(solution)/shard_map/pallas_call | solution.py:196
  189.8 4.1 %collective-permute-done.23.theirs = f32[16,128,256]{2,1,0:T(8,128)S(1)} collective-permute-done((f32[16,128,256]{2,1,0:T(8,128)S(1)}, f32[16,128,256]{2,1,0:T(8,128)S(1)}, u32[]{:S(2)}, u32[]{:S(2)}) %collective-permute-start.23) | collective-permute-done | bytes 2097184 | tf_op jit(solution)/shard_map/ppermute | solution.py:510
  194.2 13.1 %collective-permute-start.24 = (f32[4,64,256]{2,1,0:T(8,128)S(1)}, f32[4,64,256]{2,1,0:T(8,128)S(1)}, u32[]{:S(2)}, u32[]{:S(2)}) collective-permute-start(f32[4,64,256]{2,1,0:T(8,128)S(1)} %get-tuple-element.69), channel_id=1, source_target_pairs={{0,8},{8,16},{16,24},{24,0},{1,9},{9,17},{17,25},{25,1},{2,10},{10... | collective-permute-start | bytes 786440 | tf_op jit(solution)/shard_map/ppermute | solution.py:513
  207.2 3.6 %collective-permute-start.25 = (f32[4,64,256]{2,1,0:T(8,128)S(1)}, f32[4,64,256]{2,1,0:T(8,128)S(1)}, u32[]{:S(2)}, u32[]{:S(2)}) collective-permute-start(f32[4,64,256]{2,1,0:T(8,128)S(1)} %get-tuple-element.70), channel_id=1, source_target_pairs={{0,16},{8,24},{16,0},{24,8},{1,17},{9,25},{17,1},{25,9},{2,18},{10... | collective-permute-start | bytes 786440 | tf_op jit(solution)/shard_map/ppermute | solution.py:513
  215.9 6.5 %collective-permute-start.29 = (f32[4,64,256]{2,1,0:T(8,128)S(1)}, f32[4,64,256]{2,1,0:T(8,128)S(1)}, u32[]{:S(2)}, u32[]{:S(2)}) collective-permute-start(f32[4,64,256]{2,1,0:T(8,128)S(1)} %get-tuple-element.75), channel_id=1, source_target_pairs={{0,6},{2,0},{4,2},{6,4},{1,7},{3,1},{5,3},{7,5},{8,14},{10,8},{12,... | collective-permute-start | bytes 786440 | tf_op jit(solution)/shard_map/ppermute | solution.py:513
  228.5 4.1 %collective-permute-start.31 = (f32[64,256]{1,0:T(8,128)S(1)}, f32[64,256]{1,0:T(8,128)S(1)}, u32[]{:S(2)}, u32[]{:S(2)}) collective-permute-start(f32[64,256]{1,0:T(8,128)S(1)} %get-tuple-element.78), channel_id=1, source_target_pairs={{0,4},{2,6},{4,0},{6,2},{1,5},{3,7},{5,1},{7,3},{8,12},{10,14},{12... | collective-permute-start | bytes 196616 | tf_op jit(solution)/shard_map/ppermute | solution.py:513
  235.3 3.9 %collective-permute-start.34 = (f32[64,256]{1,0:T(8,128)S(1)}, f32[64,256]{1,0:T(8,128)S(1)}, u32[]{:S(2)}, u32[]{:S(2)}) collective-permute-start(f32[64,256]{1,0:T(8,128)S(1)} %get-tuple-element.82), channel_id=1, source_target_pairs={{0,16},{8,24},{16,0},{24,8},{1,17},{9,25},{17,1},{25,9},{2,18},{10... | collective-permute-start | bytes 196616 | tf_op jit(solution)/shard_map/ppermute | solution.py:513
  244.5 12.9 %all_to_all.15 = f32[32,8,256]{2,1,0:T(8,128)S(1)} all-to-all(f32[32,8,256]{2,1,0:T(8,128)S(1)} %bitcast.43), channel_id=1, replica_groups=mesh['z'=8,'x'=4,'y'=4,'core'=2] {'x','y','core'}, dimensions={0} | all-to-all | bytes 524288 | tf_op jit(solution)/shard_map/all_to_all | solution.py:523
  257.4 13.4 %all_to_all.16 = f32[8,8,256]{2,1,0:T(8,128)S(1)} all-to-all(f32[8,8,256]{2,1,0:T(8,128)S(1)} %broadcast_in_dim.106), channel_id=1, replica_groups=mesh['z'=8,'x'=4,'y'=4,'core'=2] {'z'}, dimensions={0} | all-to-all | bytes 131072 | tf_op jit(solution)/shard_map/all_to_all | solution.py:525
  270.9 12.6 %all_to_all.17 = f32[32,8,256]{2,1,0:T(8,128)} all-to-all(f32[32,8,256]{2,1,0:T(8,128)S(1)} %broadcast_in_dim.107), channel_id=1, replica_groups=mesh['z'=8,'x'=4,'y'=4,'core'=2] {'x','y','core'}, dimensions={0} | all-to-all | bytes 524288 | tf_op jit(solution)/shard_map/all_to_all | solution.py:527
  283.4 12.1 %factor.1 = (f32[256,256]{1,0:T(8,128)}, f32[128,256]{1,0:T(8,128)}) custom-call(f32[256,256]{1,0:T(8,128)} %bitcast.49, f32[256,128]{1,0:T(8,128)} %copy-done.8), custom_call_target="tpu_custom_call" | custom-call | tf_op jit(solution)/shard_map/factor/pallas_call | solution.py:381
  (125 shorter events, 66.2 us)
Async XLA Ops:
  1.5 13.8 %collective-permute-start.3 = (s32[2,128]{1,0:T(2,128)S(1)}, s32[2,128]{1,0:T(2,128)S(1)}, u32[]{:S(2)}, u32[]{:S(2)}) collective-permute-start(s32[2,128]{1,0:T(2,128)S(1)} %reshape_reshape.3.x_ref), channel_id=1, source_target_pairs={{0,8},{8,16},{16,24},{24,0},{1,9},{9,17},{17,25},{25,1},{2,10},{10... | collective-permute-start | bytes 3080 | tf_op jit(solution)/shard_map/ppermute | solution.py:443
  3.0 12.3 %collective-permute-start.4 = (s32[2,128]{1,0:T(2,128)S(1)}, s32[2,128]{1,0:T(2,128)S(1)}, u32[]{:S(2)}, u32[]{:S(2)}) collective-permute-start(s32[2,128]{1,0:T(2,128)S(1)} %reshape_reshape.3.x_ref), channel_id=1, source_target_pairs={{0,16},{8,24},{16,0},{24,8},{1,17},{9,25},{17,1},{25,9},{2,18},{10... | collective-permute-start | bytes 3080 | tf_op jit(solution)/shard_map/ppermute | solution.py:443
  8.7 30.2 %collective-permute-start.9 = (bf16[16,128,256]{2,1,0:T(8,128)(2,1)}, bf16[16,128,256]{2,1,0:T(8,128)(2,1)S(1)}, u32[]{:S(2)}, u32[]{:S(2)}) collective-permute-start(bf16[16,128,256]{2,1,0:T(8,128)(2,1)} %get-tuple-element.56), channel_id=1, source_target_pairs={{0,32},{32,64},{64,96},{96,128},{128,160},{160,192},{192,224},{224... | collective-permute-start | bytes 3145736 | tf_op jit(solution)/shard_map/ppermute | solution.py:426
  10.7 28.2 %collective-permute-start.13 = (bf16[16,128,256]{2,1,0:T(8,128)(2,1)}, bf16[16,128,256]{2,1,0:T(8,128)(2,1)}, u32[]{:S(2)}, u32[]{:S(2)}) collective-permute-start(bf16[16,128,256]{2,1,0:T(8,128)(2,1)} %get-tuple-element.57), channel_id=1, source_target_pairs={{0,224},{32,0},{64,32},{96,64},{128,96},{160,128},{192,160},{224,1... | collective-permute-start | bytes 3145736 | tf_op jit(solution)/shard_map/ppermute | solution.py:427
  23.6 37.4 %collective-permute-start.17 = (bf16[16,128,256]{2,1,0:T(8,128)(2,1)}, bf16[16,128,256]{2,1,0:T(8,128)(2,1)}, u32[]{:S(2)}, u32[]{:S(2)}) collective-permute-start(bf16[16,128,256]{2,1,0:T(8,128)(2,1)} %get-tuple-element.56), channel_id=1, source_target_pairs={{0,224},{32,0},{64,32},{96,64},{128,96},{160,128},{192,160},{224,1... | collective-permute-start | bytes 3145736 | tf_op jit(solution)/shard_map/ppermute | solution.py:427
  25.6 35.8 %collective-permute-start.20 = (bf16[16,128,256]{2,1,0:T(8,128)(2,1)}, bf16[16,128,256]{2,1,0:T(8,128)(2,1)}, u32[]{:S(2)}, u32[]{:S(2)}) collective-permute-start(bf16[16,128,256]{2,1,0:T(8,128)(2,1)} %get-tuple-element.57), channel_id=1, source_target_pairs={{0,32},{32,64},{64,96},{96,128},{128,160},{160,192},{192,224},{224... | collective-permute-start | bytes 3145736 | tf_op jit(solution)/shard_map/ppermute | solution.py:426
  38.8 43.4 %collective-permute-start.10 = (bf16[16,128,256]{2,1,0:T(8,128)(2,1)S(1)}, bf16[16,128,256]{2,1,0:T(8,128)(2,1)}, u32[]{:S(2)}, u32[]{:S(2)}) collective-permute-start(bf16[16,128,256]{2,1,0:T(8,128)(2,1)S(1)} %collective-permute-done.9.refs_13_), channel_id=1, source_target_pairs={{0,32},{32,64},{64,96},{96,128},{128,160},{160,192},{192,224},{224... | collective-permute-start | bytes 3145736 | tf_op jit(solution)/shard_map/ppermute | solution.py:455
  38.8 44.7 %collective-permute-start.14 = (bf16[16,128,256]{2,1,0:T(8,128)(2,1)}, bf16[16,128,256]{2,1,0:T(8,128)(2,1)}, u32[]{:S(2)}, u32[]{:S(2)}) collective-permute-start(bf16[16,128,256]{2,1,0:T(8,128)(2,1)} %collective-permute-done.13.refs_12_), channel_id=1, source_target_pairs={{0,224},{32,0},{64,32},{96,64},{128,96},{160,128},{192,160},{224,1... | collective-permute-start | bytes 3145736 | tf_op jit(solution)/shard_map/ppermute | solution.py:457
  52.0 56.2 %collective-permute-start.6 = (bf16[72,128,128]{2,1,0:T(8,128)(2,1)}, bf16[72,128,128]{2,1,0:T(8,128)(2,1)S(1)}, u32[]{:S(2)}, u32[]{:S(2)}) collective-permute-start(bf16[72,128,128]{2,1,0:T(8,128)(2,1)} %get-tuple-element.53), channel_id=1, source_target_pairs={{0,8},{8,16},{16,24},{24,0},{1,9},{9,17},{17,25},{25,1},{2,10},{10... | collective-permute-start | bytes 7077896 | tf_op jit(solution)/shard_map/ppermute | solution.py:447
  61.0 56.0 %collective-permute-start.7 = (bf16[72,128,128]{2,1,0:T(8,128)(2,1)}, bf16[72,128,128]{2,1,0:T(8,128)(2,1)}, u32[]{:S(2)}, u32[]{:S(2)}) collective-permute-start(bf16[72,128,128]{2,1,0:T(8,128)(2,1)} %get-tuple-element.54), channel_id=1, source_target_pairs={{0,16},{8,24},{16,0},{24,8},{1,17},{9,25},{17,1},{25,9},{2,18},{10... | collective-permute-start | bytes 7077896 | tf_op jit(solution)/shard_map/ppermute | solution.py:447
  61.4 42.6 %collective-permute-start.18 = (bf16[16,128,256]{2,1,0:T(8,128)(2,1)}, bf16[16,128,256]{2,1,0:T(8,128)(2,1)}, u32[]{:S(2)}, u32[]{:S(2)}) collective-permute-start(bf16[16,128,256]{2,1,0:T(8,128)(2,1)} %collective-permute-done.17.refs_11_), channel_id=1, source_target_pairs={{0,224},{32,0},{64,32},{96,64},{128,96},{160,128},{192,160},{224,1... | collective-permute-start | bytes 3145736 | tf_op jit(solution)/shard_map/ppermute | solution.py:457
  82.2 25.2 %collective-permute-start.21 = (bf16[16,128,256]{2,1,0:T(8,128)(2,1)}, bf16[16,128,256]{2,1,0:T(8,128)(2,1)}, u32[]{:S(2)}, u32[]{:S(2)}) collective-permute-start(bf16[16,128,256]{2,1,0:T(8,128)(2,1)} %collective-permute-done.20.refs_14_), channel_id=1, source_target_pairs={{0,32},{32,64},{64,96},{96,128},{128,160},{160,192},{192,224},{224... | collective-permute-start | bytes 3145736 | tf_op jit(solution)/shard_map/ppermute | solution.py:455
  83.5 79.2 %collective-permute-start.8 = (bf16[72,128,128]{2,1,0:T(8,128)(2,1)}, bf16[72,128,128]{2,1,0:T(8,128)(2,1)}, u32[]{:S(2)}, u32[]{:S(2)}) collective-permute-start(bf16[72,128,128]{2,1,0:T(8,128)(2,1)} %get-tuple-element.55), channel_id=1, source_target_pairs={{0,24},{8,0},{16,8},{24,16},{1,25},{9,1},{17,9},{25,17},{2,26},{10... | collective-permute-start | bytes 7077896 | tf_op jit(solution)/shard_map/ppermute | solution.py:447
  104.0 28.0 %collective-permute-start.11 = (bf16[16,128,256]{2,1,0:T(8,128)(2,1)}, bf16[16,128,256]{2,1,0:T(8,128)(2,1)}, u32[]{:S(2)}, u32[]{:S(2)}) collective-permute-start(bf16[16,128,256]{2,1,0:T(8,128)(2,1)} %collective-permute-done.10.refs_17_), channel_id=1, source_target_pairs={{0,32},{32,64},{64,96},{96,128},{128,160},{160,192},{192,224},{224... | collective-permute-start | bytes 3145736 | tf_op jit(solution)/shard_map/ppermute | solution.py:455
  107.4 26.3 %collective-permute-start.15 = (bf16[16,128,256]{2,1,0:T(8,128)(2,1)}, bf16[16,128,256]{2,1,0:T(8,128)(2,1)}, u32[]{:S(2)}, u32[]{:S(2)}) collective-permute-start(bf16[16,128,256]{2,1,0:T(8,128)(2,1)} %collective-permute-done.14.refs_16_), channel_id=1, source_target_pairs={{0,224},{32,0},{64,32},{96,64},{128,96},{160,128},{192,160},{224,1... | collective-permute-start | bytes 3145736 | tf_op jit(solution)/shard_map/ppermute | solution.py:457
  108.2 68.2 %collective-permute-start.19 = (bf16[16,128,256]{2,1,0:T(8,128)(2,1)}, bf16[16,128,256]{2,1,0:T(8,128)(2,1)S(1)}, u32[]{:S(2)}, u32[]{:S(2)}) collective-permute-start(bf16[16,128,256]{2,1,0:T(8,128)(2,1)} %collective-permute-done.18.refs_15_), channel_id=1, source_target_pairs={{0,224},{32,0},{64,32},{96,64},{128,96},{160,128},{192,160},{224,1... | collective-permute-start | bytes 3145736 | tf_op jit(solution)/shard_map/ppermute | solution.py:457
  117.0 60.4 %collective-permute-start.22 = (bf16[16,128,256]{2,1,0:T(8,128)(2,1)}, bf16[16,128,256]{2,1,0:T(8,128)(2,1)S(1)}, u32[]{:S(2)}, u32[]{:S(2)}) collective-permute-start(bf16[16,128,256]{2,1,0:T(8,128)(2,1)} %collective-permute-done.21.refs_18_), channel_id=1, source_target_pairs={{0,32},{32,64},{64,96},{96,128},{128,160},{160,192},{192,224},{224... | collective-permute-start | bytes 3145736 | tf_op jit(solution)/shard_map/ppermute | solution.py:455
  132.0 52.0 %collective-permute-start.12 = (bf16[16,128,256]{2,1,0:T(8,128)(2,1)}, bf16[16,128,256]{2,1,0:T(8,128)(2,1)S(1)}, u32[]{:S(2)}, u32[]{:S(2)}) collective-permute-start(bf16[16,128,256]{2,1,0:T(8,128)(2,1)} %collective-permute-done.11.refs_8_), channel_id=1, source_target_pairs={{0,32},{32,64},{64,96},{96,128},{128,160},{160,192},{192,224},{224... | collective-permute-start | bytes 3145736 | tf_op jit(solution)/shard_map/ppermute | solution.py:455
  133.7 51.3 %collective-permute-start.16 = (bf16[16,128,256]{2,1,0:T(8,128)(2,1)}, bf16[16,128,256]{2,1,0:T(8,128)(2,1)}, u32[]{:S(2)}, u32[]{:S(2)}) collective-permute-start(bf16[16,128,256]{2,1,0:T(8,128)(2,1)} %collective-permute-done.15.refs_7_), channel_id=1, source_target_pairs={{0,224},{32,0},{64,32},{96,64},{128,96},{160,128},{192,160},{224,1... | collective-permute-start | bytes 3145736 | tf_op jit(solution)/shard_map/ppermute | solution.py:457
  194.2 21.8 %collective-permute-start.24 = (f32[4,64,256]{2,1,0:T(8,128)S(1)}, f32[4,64,256]{2,1,0:T(8,128)S(1)}, u32[]{:S(2)}, u32[]{:S(2)}) collective-permute-start(f32[4,64,256]{2,1,0:T(8,128)S(1)} %get-tuple-element.69), channel_id=1, source_target_pairs={{0,8},{8,16},{16,24},{24,0},{1,9},{9,17},{17,25},{25,1},{2,10},{10... | collective-permute-start | bytes 786440 | tf_op jit(solution)/shard_map/ppermute | solution.py:513
  207.2 15.2 %collective-permute-start.25 = (f32[4,64,256]{2,1,0:T(8,128)S(1)}, f32[4,64,256]{2,1,0:T(8,128)S(1)}, u32[]{:S(2)}, u32[]{:S(2)}) collective-permute-start(f32[4,64,256]{2,1,0:T(8,128)S(1)} %get-tuple-element.70), channel_id=1, source_target_pairs={{0,16},{8,24},{16,0},{24,8},{1,17},{9,25},{17,1},{25,9},{2,18},{10... | collective-permute-start | bytes 786440 | tf_op jit(solution)/shard_map/ppermute | solution.py:513
  210.8 11.9 %collective-permute-start.26 = (f32[4,64,256]{2,1,0:T(8,128)S(1)}, f32[4,64,256]{2,1,0:T(8,128)S(1)}, u32[]{:S(2)}, u32[]{:S(2)}) collective-permute-start(f32[4,64,256]{2,1,0:T(8,128)S(1)} %get-tuple-element.71), channel_id=1, source_target_pairs={{0,24},{8,0},{16,8},{24,16},{1,25},{9,1},{17,9},{25,17},{2,26},{10... | collective-permute-start | bytes 786440 | tf_op jit(solution)/shard_map/ppermute | solution.py:513
  210.8 11.9 %collective-permute-start.27 = (f32[4,64,256]{2,1,0:T(8,128)S(1)}, f32[4,64,256]{2,1,0:T(8,128)S(1)}, u32[]{:S(2)}, u32[]{:S(2)}) collective-permute-start(f32[4,64,256]{2,1,0:T(8,128)S(1)} %get-tuple-element.73), channel_id=1, source_target_pairs={{0,2},{2,4},{4,6},{6,0},{1,3},{3,5},{5,7},{7,1},{8,10},{10,12},{12... | collective-permute-start | bytes 786440 | tf_op jit(solution)/shard_map/ppermute | solution.py:513
  213.3 12.6 %collective-permute-start.28 = (f32[4,64,256]{2,1,0:T(8,128)S(1)}, f32[4,64,256]{2,1,0:T(8,128)S(1)}, u32[]{:S(2)}, u32[]{:S(2)}) collective-permute-start(f32[4,64,256]{2,1,0:T(8,128)S(1)} %get-tuple-element.74), channel_id=1, source_target_pairs={{0,4},{2,6},{4,0},{6,2},{1,5},{3,7},{5,1},{7,3},{8,12},{10,14},{12... | collective-permute-start | bytes 786440 | tf_op jit(solution)/shard_map/ppermute | solution.py:513
  (21 other events, 197.5 us)

commit v2 on v1

--- a/solution.py
+++ b/solution.py
@@ -236,7 +236,7 @@
 def add_up_kernel(*refs):
     outs = refs[2 * NX :]
     for side in range(2):
-        ins = refs[side * NX : (side + 1) * NX]
+        ins = refs[side : 2 * NX : 2]
         for r in range(NX):
             outs[side * NX + r][...] = (ins[0][r] + ins[1][r]) + (ins[2][r] + ins[3][r])
 
@@ -253,11 +253,15 @@
     return out[:NX], out[NX:]
 
 
+def in_turn(top, bottom):
+    return [side[r] for r in (2, 1, 3, 0) for side in (top, bottom)]
+
+
 def local_gram_kernel(*refs):
     gram, image_t = refs[2 * NX :]
     sides = [
         (side[0][...] + side[1][...]) + (side[2][...] + side[3][...])
-        for side in (refs[:NX], refs[NX : 2 * NX])
+        for side in (refs[: 2 * NX : 2], refs[1 : 2 * NX : 2])
     ]
     image = jnp.concatenate(sides, axis=0)
     image_t[...] = image.T
@@ -278,7 +282,7 @@
         out_specs=[vm, vm],
         compiler_params=pltpu.CompilerParams(vmem_limit_bytes=16 << 20),
         name="local_gram",
-    )(*top, *bottom)
+    )(*in_turn(top, bottom))
 
 
 def spread(mine, theirs):
@@ -286,7 +290,7 @@
 
 
 def add_up(top, bottom):
-    return in_vmem(add_up_kernel, (*top, *bottom), (BS // 2, K))
+    return in_vmem(add_up_kernel, in_turn(top, bottom), (BS // 2, K))
 
 
 def factor_block(d):
@@ -509,10 +513,10 @@
     mine, other = prev
     parts = spread(mine, lax.ppermute(other, "core", ring(NC, 1)))
     for axes in (("x", "y"), ("y", "x")):
-        moved = [
-            [part if r == 0 else lax.ppermute(part, axis, ring(NX, r)) for r, part in enumerate(side)]
-            for axis, side in zip(axes, parts)
-        ]
+        moved = [list(side) for side in parts]
+        for r in (2, 1, 3):
+            for axis, side in zip(axes, moved):
+                side[r] = lax.ppermute(side[r], axis, ring(NX, r))
         if axes[0] == "x":
             parts = add_up(*moved)
     gram, image_t = local_gram(*moved)

time: 298 us -> 294 us (0.987)
  starting transfers between devices: 65 us -> 61.5 us
    ppermute x12, starting transfers between devices: 38.7 us -> 35.2 us  [one_device(): side[r] = lax.ppermute(side[r], axis, ring(NX, r))]
  transfers between devices with their start and end apart: 33 -> 33, of which waited for: 19 -> 17; matrix products, arithmetic and copies ran while one was open for 3% -> 3% of each run, Pallas kernels for 12% -> 12%
where the time goes in v2:
time: 294 us; the launch traced here: 291 us
  waiting for transfers between devices  121 us (41%)
  starting transfers between devices  61.5 us (21%)
  Pallas kernels  51.7 us (18%)
  blocking collectives  40.1 us (14%)
  local copies, waits for them, and re-layouts  10.3 us (4%)
  other arithmetic  5.43 us (2%)
    ppermute x12, starting transfers between devices, one_device(): side[r] = lax.ppermute(side[r], axis, ring(NX, r))  35.2 us
    ppermute x5, waiting for transfers between devices, one_device(): fwd[step][h] = lax.ppermute(fwd[step - 1][h], 'z', ring(NZ, 1))  34.9 us
    ppermute x3, waiting for transfers between devices, one_device(): vals[dx] = lax.ppermute(vals[dx], 'x', ring(NX, dx))  28.7 us
    pallas_call x3, Pallas kernels, products(): pl.pallas_call(functools.partial(products_kernel, ds, halves, window, fir...  22.4 us
    ppermute x5, waiting for transfers between devices, one_device(): bwd[step][h] = lax.ppermute(bwd[step - 1][h], 'z', ring(NZ, -1))  22.1 us
    all_to_all x1, blocking collectives, one_device(): part = jnp.sum(lax.all_to_all(gram, plane, 0, 0, tiled=True), axis=0)  14 us
    all_to_all x1, blocking collectives, one_device(): lax.all_to_all(part, 'z', 0, 0, tiled=True)  13.5 us
    ppermute x2, waiting for transfers between devices, one_device(): fwd = {1: [lax.ppermute(blocks[h], 'z', ring(NZ, 1)) for h in range(2)]}  13.3 us
  transfers between devices with their start and end apart: 33, of which 17 were waited for; matrix products, arithmetic and copies ran while one was open for 3% of the time, Pallas kernels for 12%

profile of v2, /device:TPU:2, one launch (start us, length us, event | category | flops | bytes accessed | tf_op | source)
XLA Modules:
  0.0 291.5 jit_solution(11407618661770979383)
XLA Ops:
  10.7 4.0 %collective-permute-start.13 = (bf16[16,128,256]{2,1,0:T(8,128)(2,1)}, bf16[16,128,256]{2,1,0:T(8,128)(2,1)}, u32[]{:S(2)}, u32[]{:S(2)}) collective-permute-start(bf16[16,128,256]{2,1,0:T(8,128)(2,1)} %get-tuple-element.57), channel_id=1, source_target_pairs={{0,224},{32,0},{64,32},{96,64},{128,96},{160,128},{192,160},{224,1... | collective-permute-start | bytes 3145736 | tf_op jit(solution)/shard_map/ppermute | solution.py:431
  20.2 3.4 %conditional.1 = (bf16[24,128,128]{2,1,0:T(8,128)(2,1)S(1)}, bf16[24,128,128]{2,1,0:T(8,128)(2,1)}, bf16[24,128,128]{2,1,0:T(8,128)(2,1)}, bf16[24,128,128]{2,1,0:T(8,128)(2,1)}) conditional(s32[]{:T(128)} %convert_element_type.19, () %tuple.18, (s32[4,96]{1,0:T(4,128)S(1)}, bf16[256,128,128]{2,1,0:T(8,128)(2,1)}) %tuple.35), branch_computations={%region_10.11_spmd, %region_11.12_spmd} | conditional | flops 4384 | bytes 15746712 | solution.py:506
  25.7 13.2 %collective-permute-done.9.refs_13_ = bf16[16,128,256]{2,1,0:T(8,128)(2,1)S(1)} collective-permute-done((bf16[16,128,256]{2,1,0:T(8,128)(2,1)}, bf16[16,128,256]{2,1,0:T(8,128)(2,1)S(1)}, u32[]{:S(2)}, u32[]{:S(2)}) %collective-permute-start.9) | collective-permute-done | bytes 1048608 | tf_op jit(solution)/shard_map/ppermute | solution.py:430
  38.8 3.4 %collective-permute-start.14 = (bf16[16,128,256]{2,1,0:T(8,128)(2,1)}, bf16[16,128,256]{2,1,0:T(8,128)(2,1)}, u32[]{:S(2)}, u32[]{:S(2)}) collective-permute-start(bf16[16,128,256]{2,1,0:T(8,128)(2,1)} %collective-permute-done.13.refs_12_), channel_id=1, source_target_pairs={{0,224},{32,0},{64,32},{96,64},{128,96},{160,128},{192,160},{224,1... | collective-permute-start | bytes 3145736 | tf_op jit(solution)/shard_map/ppermute | solution.py:461
  42.3 9.6 %shard_map.60 = (bf16[72,128,128]{2,1,0:T(8,128)(2,1)}, bf16[72,128,128]{2,1,0:T(8,128)(2,1)}, bf16[72,128,128]{2,1,0:T(8,128)(2,1)}) custom-call(s32[216]{0:T(256)S(1)} %reshape.1294.index, bf16[256,128,128]{2,1,0:T(8,128)(2,1)} %bitcast.45), custom_call_target="tpu_custom_call" | custom-call | bytes 14155776 | tf_op jit(solution)/shard_map/pallas_call | solution.py:87
  52.1 9.0 %collective-permute-done.17.refs_11_ = bf16[16,128,256]{2,1,0:T(8,128)(2,1)} collective-permute-done((bf16[16,128,256]{2,1,0:T(8,128)(2,1)}, bf16[16,128,256]{2,1,0:T(8,128)(2,1)}, u32[]{:S(2)}, u32[]{:S(2)}) %collective-permute-start.17) | collective-permute-done | bytes 1048608 | tf_op jit(solution)/shard_map/ppermute | solution.py:431
  61.4 3.6 %collective-permute-start.18 = (bf16[16,128,256]{2,1,0:T(8,128)(2,1)}, bf16[16,128,256]{2,1,0:T(8,128)(2,1)}, u32[]{:S(2)}, u32[]{:S(2)}) collective-permute-start(bf16[16,128,256]{2,1,0:T(8,128)(2,1)} %collective-permute-done.17.refs_11_), channel_id=1, source_target_pairs={{0,224},{32,0},{64,32},{96,64},{128,96},{160,128},{192,160},{224,1... | collective-permute-start | bytes 3145736 | tf_op jit(solution)/shard_map/ppermute | solution.py:461
  65.0 17.2 %collective-permute-done.10.refs_17_ = bf16[16,128,256]{2,1,0:T(8,128)(2,1)} collective-permute-done((bf16[16,128,256]{2,1,0:T(8,128)(2,1)S(1)}, bf16[16,128,256]{2,1,0:T(8,128)(2,1)}, u32[]{:S(2)}, u32[]{:S(2)}) %collective-permute-start.10) | collective-permute-done | bytes 1048608 | tf_op jit(solution)/shard_map/ppermute | solution.py:459
  84.9 19.1 %collective-permute-done.18.refs_15_ = bf16[16,128,256]{2,1,0:T(8,128)(2,1)} collective-permute-done((bf16[16,128,256]{2,1,0:T(8,128)(2,1)}, bf16[16,128,256]{2,1,0:T(8,128)(2,1)}, u32[]{:S(2)}, u32[]{:S(2)}) %collective-permute-start.18) | collective-permute-done | bytes 1048608 | tf_op jit(solution)/shard_map/ppermute | solution.py:461
  110.3 6.7 %collective-permute-done.7.refs_4_ = bf16[72,128,128]{2,1,0:T(8,128)(2,1)} collective-permute-done((bf16[72,128,128]{2,1,0:T(8,128)(2,1)}, bf16[72,128,128]{2,1,0:T(8,128)(2,1)}, u32[]{:S(2)}, u32[]{:S(2)}) %collective-permute-start.7) | collective-permute-done | bytes 2359328 | tf_op jit(solution)/shard_map/ppermute | solution.py:451
  117.4 14.6 %collective-permute-done.11.refs_8_ = bf16[16,128,256]{2,1,0:T(8,128)(2,1)} collective-permute-done((bf16[16,128,256]{2,1,0:T(8,128)(2,1)}, bf16[16,128,256]{2,1,0:T(8,128)(2,1)}, u32[]{:S(2)}, u32[]{:S(2)}) %collective-permute-start.11) | collective-permute-done | bytes 1048608 | tf_op jit(solution)/shard_map/ppermute | solution.py:459
  135.3 3.2 %shard_map.59.refs_2_ = bf16[72,128,128]{2,1,0:T(8,128)(2,1)S(1)} custom-call(s32[72]{0:T(128)S(1)} %slice_bitcast_fusion.index, bf16[256,128,128]{2,1,0:T(8,128)(2,1)} %bitcast.46), custom_call_target="tpu_custom_call" | custom-call | bytes 4718592 | tf_op jit(solution)/shard_map/pallas_call | solution.py:87
  140.8 22.0 %collective-permute-done.8.refs_5_ = bf16[72,128,128]{2,1,0:T(8,128)(2,1)} collective-permute-done((bf16[72,128,128]{2,1,0:T(8,128)(2,1)}, bf16[72,128,128]{2,1,0:T(8,128)(2,1)}, u32[]{:S(2)}, u32[]{:S(2)}) %collective-permute-start.8) | collective-permute-done | bytes 2359328 | tf_op jit(solution)/shard_map/ppermute | solution.py:451
  162.7 13.7 %shard_map.61 = (f32[16,128,256]{2,1,0:T(8,128)S(1)}, f32[16,128,256]{2,1,0:T(8,128)S(1)}) custom-call(s32[768]{0:T(1024)S(1)} %broadcast_add_fusion.refs_0_, s32[17]{0:T(128)S(1)} %pad_add_fusion.1.refs_1_, bf16[72,128,128]{2,1,0:T(8,128)(2,1)} %copy-done, bf16[72,128,128]{2,1,0:T(8,128)(2,1)} %copy-done.2, ...), custom_call_target="tpu_custom_call" | custom-call | flops 838860800 | bytes 23068672 | tf_op jit(solution)/shard_map/pallas_call | solution.py:196
  178.7 5.3 %shard_map.62 = (f32[16,128,256]{2,1,0:T(8,128)S(1)}, f32[16,128,256]{2,1,0:T(8,128)S(1)}) custom-call(s32[768]{0:T(1024)S(1)} %broadcast_add_fusion.refs_0_, s32[17]{0:T(128)S(1)} %pad_add_fusion.1.refs_1_, bf16[72,128,128]{2,1,0:T(8,128)(2,1)S(1)} %copy-done.1, ...), custom_call_target="tpu_custom_call", output_to_operand_aliasing={{0}: (10, {}), {1}: (11, {})} | custom-call | flops 335544320 | bytes 8912896 | tf_op jit(solution)/shard_map/pallas_call | solution.py:196
  186.2 3.4 %shard_map.63 = (f32[16,128,256]{2,1,0:T(8,128)S(1)}, f32[16,128,256]{2,1,0:T(8,128)S(1)}) custom-call(s32[768]{0:T(1024)S(1)} %broadcast_add_fusion.refs_0_, s32[17]{0:T(128)S(1)} %pad_add_fusion.1.refs_1_, bf16[72,128,128]{2,1,0:T(8,128)(2,1)S(1)} %copy-done.1, bf16[72,128,128]{2,1,0:T(8,128)(2,1)S(1)} %copy-done.3, ...), custom_call_target="tpu_custom_call", output_to_operand_aliasing={{0}: (8, {}), {1}: (9, {})} | custom-call | flops 167772160 | bytes 3670016 | tf_op jit(solution)/shard_map/pallas_call | solution.py:196
  189.8 4.1 %collective-permute-done.23.theirs = f32[16,128,256]{2,1,0:T(8,128)S(1)} collective-permute-done((f32[16,128,256]{2,1,0:T(8,128)S(1)}, f32[16,128,256]{2,1,0:T(8,128)S(1)}, u32[]{:S(2)}, u32[]{:S(2)}) %collective-permute-start.23) | collective-permute-done | bytes 2097184 | tf_op jit(solution)/shard_map/ppermute | solution.py:514
  198.2 14.9 %collective-permute-start.26 = (f32[4,64,256]{2,1,0:T(8,128)S(1)}, f32[4,64,256]{2,1,0:T(8,128)S(1)}, u32[]{:S(2)}, u32[]{:S(2)}) collective-permute-start(f32[4,64,256]{2,1,0:T(8,128)S(1)} %get-tuple-element.70), channel_id=1, source_target_pairs={{0,8},{8,16},{16,24},{24,0},{1,9},{9,17},{17,25},{25,1},{2,10},{10... | collective-permute-start | bytes 786440 | tf_op jit(solution)/shard_map/ppermute | solution.py:519
  216.9 4.4 %collective-permute-done.26.refs_2_ = f32[4,64,256]{2,1,0:T(8,128)S(1)} collective-permute-done((f32[4,64,256]{2,1,0:T(8,128)S(1)}, f32[4,64,256]{2,1,0:T(8,128)S(1)}, u32[]{:S(2)}, u32[]{:S(2)}) %collective-permute-start.26) | collective-permute-done | bytes 262176 | tf_op jit(solution)/shard_map/ppermute | solution.py:519
  221.9 3.9 %collective-permute-start.30 = (f32[64,256]{1,0:T(8,128)S(1)}, f32[64,256]{1,0:T(8,128)S(1)}, u32[]{:S(2)}, u32[]{:S(2)}) collective-permute-start(f32[64,256]{1,0:T(8,128)S(1)} %get-tuple-element.76), channel_id=1, source_target_pairs={{0,4},{2,6},{4,0},{6,2},{1,5},{3,7},{5,1},{7,3},{8,12},{10,14},{12... | collective-permute-start | bytes 196616 | tf_op jit(solution)/shard_map/ppermute | solution.py:519
  239.2 14.0 %all_to_all.15 = f32[32,8,256]{2,1,0:T(8,128)S(1)} all-to-all(f32[32,8,256]{2,1,0:T(8,128)S(1)} %bitcast.43), channel_id=1, replica_groups=mesh['z'=8,'x'=4,'y'=4,'core'=2] {'x','y','core'}, dimensions={0} | all-to-all | bytes 524288 | tf_op jit(solution)/shard_map/all_to_all | solution.py:527
  253.3 13.5 %all_to_all.16 = f32[8,8,256]{2,1,0:T(8,128)S(1)} all-to-all(f32[8,8,256]{2,1,0:T(8,128)S(1)} %broadcast_in_dim.106), channel_id=1, replica_groups=mesh['z'=8,'x'=4,'y'=4,'core'=2] {'z'}, dimensions={0} | all-to-all | bytes 131072 | tf_op jit(solution)/shard_map/all_to_all | solution.py:529
  266.9 12.6 %all_to_all.17 = f32[32,8,256]{2,1,0:T(8,128)} all-to-all(f32[32,8,256]{2,1,0:T(8,128)S(1)} %broadcast_in_dim.107), channel_id=1, replica_groups=mesh['z'=8,'x'=4,'y'=4,'core'=2] {'x','y','core'}, dimensions={0} | all-to-all | bytes 524288 | tf_op jit(solution)/shard_map/all_to_all | solution.py:531
  279.4 12.1 %factor.1 = (f32[256,256]{1,0:T(8,128)}, f32[128,256]{1,0:T(8,128)}) custom-call(f32[256,256]{1,0:T(8,128)} %bitcast.49, f32[256,128]{1,0:T(8,128)} %copy-done.8), custom_call_target="tpu_custom_call" | custom-call | tf_op jit(solution)/shard_map/factor/pallas_call | solution.py:385
  (125 shorter events, 62.4 us)
Async XLA Ops:
  1.5 13.8 %collective-permute-start.3 = (s32[2,128]{1,0:T(2,128)S(1)}, s32[2,128]{1,0:T(2,128)S(1)}, u32[]{:S(2)}, u32[]{:S(2)}) collective-permute-start(s32[2,128]{1,0:T(2,128)S(1)} %reshape_reshape.3.x_ref), channel_id=1, source_target_pairs={{0,8},{8,16},{16,24},{24,0},{1,9},{9,17},{17,25},{25,1},{2,10},{10... | collective-permute-start | bytes 3080 | tf_op jit(solution)/shard_map/ppermute | solution.py:447
  3.0 12.3 %collective-permute-start.4 = (s32[2,128]{1,0:T(2,128)S(1)}, s32[2,128]{1,0:T(2,128)S(1)}, u32[]{:S(2)}, u32[]{:S(2)}) collective-permute-start(s32[2,128]{1,0:T(2,128)S(1)} %reshape_reshape.3.x_ref), channel_id=1, source_target_pairs={{0,16},{8,24},{16,0},{24,8},{1,17},{9,25},{17,1},{25,9},{2,18},{10... | collective-permute-start | bytes 3080 | tf_op jit(solution)/shard_map/ppermute | solution.py:447
  5.8 9.5 %collective-permute-start.5 = (s32[2,128]{1,0:T(2,128)S(1)}, s32[2,128]{1,0:T(2,128)S(1)}, u32[]{:S(2)}, u32[]{:S(2)}) collective-permute-start(s32[2,128]{1,0:T(2,128)S(1)} %reshape_reshape.3.x_ref), channel_id=1, source_target_pairs={{0,24},{8,0},{16,8},{24,16},{1,25},{9,1},{17,9},{25,17},{2,26},{10... | collective-permute-start | bytes 3080 | tf_op jit(solution)/shard_map/ppermute | solution.py:447
  8.7 30.2 %collective-permute-start.9 = (bf16[16,128,256]{2,1,0:T(8,128)(2,1)}, bf16[16,128,256]{2,1,0:T(8,128)(2,1)S(1)}, u32[]{:S(2)}, u32[]{:S(2)}) collective-permute-start(bf16[16,128,256]{2,1,0:T(8,128)(2,1)} %get-tuple-element.56), channel_id=1, source_target_pairs={{0,32},{32,64},{64,96},{96,128},{128,160},{160,192},{192,224},{224... | collective-permute-start | bytes 3145736 | tf_op jit(solution)/shard_map/ppermute | solution.py:430
  10.7 28.2 %collective-permute-start.13 = (bf16[16,128,256]{2,1,0:T(8,128)(2,1)}, bf16[16,128,256]{2,1,0:T(8,128)(2,1)}, u32[]{:S(2)}, u32[]{:S(2)}) collective-permute-start(bf16[16,128,256]{2,1,0:T(8,128)(2,1)} %get-tuple-element.57), channel_id=1, source_target_pairs={{0,224},{32,0},{64,32},{96,64},{128,96},{160,128},{192,160},{224,1... | collective-permute-start | bytes 3145736 | tf_op jit(solution)/shard_map/ppermute | solution.py:431
  23.6 37.4 %collective-permute-start.17 = (bf16[16,128,256]{2,1,0:T(8,128)(2,1)}, bf16[16,128,256]{2,1,0:T(8,128)(2,1)}, u32[]{:S(2)}, u32[]{:S(2)}) collective-permute-start(bf16[16,128,256]{2,1,0:T(8,128)(2,1)} %get-tuple-element.56), channel_id=1, source_target_pairs={{0,224},{32,0},{64,32},{96,64},{128,96},{160,128},{192,160},{224,1... | collective-permute-start | bytes 3145736 | tf_op jit(solution)/shard_map/ppermute | solution.py:431
  25.6 35.8 %collective-permute-start.20 = (bf16[16,128,256]{2,1,0:T(8,128)(2,1)}, bf16[16,128,256]{2,1,0:T(8,128)(2,1)}, u32[]{:S(2)}, u32[]{:S(2)}) collective-permute-start(bf16[16,128,256]{2,1,0:T(8,128)(2,1)} %get-tuple-element.57), channel_id=1, source_target_pairs={{0,32},{32,64},{64,96},{96,128},{128,160},{160,192},{192,224},{224... | collective-permute-start | bytes 3145736 | tf_op jit(solution)/shard_map/ppermute | solution.py:430
  38.8 43.4 %collective-permute-start.10 = (bf16[16,128,256]{2,1,0:T(8,128)(2,1)S(1)}, bf16[16,128,256]{2,1,0:T(8,128)(2,1)}, u32[]{:S(2)}, u32[]{:S(2)}) collective-permute-start(bf16[16,128,256]{2,1,0:T(8,128)(2,1)S(1)} %collective-permute-done.9.refs_13_), channel_id=1, source_target_pairs={{0,32},{32,64},{64,96},{96,128},{128,160},{160,192},{192,224},{224... | collective-permute-start | bytes 3145736 | tf_op jit(solution)/shard_map/ppermute | solution.py:459
  38.8 44.7 %collective-permute-start.14 = (bf16[16,128,256]{2,1,0:T(8,128)(2,1)}, bf16[16,128,256]{2,1,0:T(8,128)(2,1)}, u32[]{:S(2)}, u32[]{:S(2)}) collective-permute-start(bf16[16,128,256]{2,1,0:T(8,128)(2,1)} %collective-permute-done.13.refs_12_), channel_id=1, source_target_pairs={{0,224},{32,0},{64,32},{96,64},{128,96},{160,128},{192,160},{224,1... | collective-permute-start | bytes 3145736 | tf_op jit(solution)/shard_map/ppermute | solution.py:461
  52.0 56.2 %collective-permute-start.6 = (bf16[72,128,128]{2,1,0:T(8,128)(2,1)}, bf16[72,128,128]{2,1,0:T(8,128)(2,1)S(1)}, u32[]{:S(2)}, u32[]{:S(2)}) collective-permute-start(bf16[72,128,128]{2,1,0:T(8,128)(2,1)} %get-tuple-element.53), channel_id=1, source_target_pairs={{0,8},{8,16},{16,24},{24,0},{1,9},{9,17},{17,25},{25,1},{2,10},{10... | collective-permute-start | bytes 7077896 | tf_op jit(solution)/shard_map/ppermute | solution.py:451
  61.0 56.0 %collective-permute-start.7 = (bf16[72,128,128]{2,1,0:T(8,128)(2,1)}, bf16[72,128,128]{2,1,0:T(8,128)(2,1)}, u32[]{:S(2)}, u32[]{:S(2)}) collective-permute-start(bf16[72,128,128]{2,1,0:T(8,128)(2,1)} %get-tuple-element.54), channel_id=1, source_target_pairs={{0,16},{8,24},{16,0},{24,8},{1,17},{9,25},{17,1},{25,9},{2,18},{10... | collective-permute-start | bytes 7077896 | tf_op jit(solution)/shard_map/ppermute | solution.py:451
  61.4 42.6 %collective-permute-start.18 = (bf16[16,128,256]{2,1,0:T(8,128)(2,1)}, bf16[16,128,256]{2,1,0:T(8,128)(2,1)}, u32[]{:S(2)}, u32[]{:S(2)}) collective-permute-start(bf16[16,128,256]{2,1,0:T(8,128)(2,1)} %collective-permute-done.17.refs_11_), channel_id=1, source_target_pairs={{0,224},{32,0},{64,32},{96,64},{128,96},{160,128},{192,160},{224,1... | collective-permute-start | bytes 3145736 | tf_op jit(solution)/shard_map/ppermute | solution.py:461
  82.2 25.2 %collective-permute-start.21 = (bf16[16,128,256]{2,1,0:T(8,128)(2,1)}, bf16[16,128,256]{2,1,0:T(8,128)(2,1)}, u32[]{:S(2)}, u32[]{:S(2)}) collective-permute-start(bf16[16,128,256]{2,1,0:T(8,128)(2,1)} %collective-permute-done.20.refs_14_), channel_id=1, source_target_pairs={{0,32},{32,64},{64,96},{96,128},{128,160},{160,192},{192,224},{224... | collective-permute-start | bytes 3145736 | tf_op jit(solution)/shard_map/ppermute | solution.py:459
  83.5 79.2 %collective-permute-start.8 = (bf16[72,128,128]{2,1,0:T(8,128)(2,1)}, bf16[72,128,128]{2,1,0:T(8,128)(2,1)}, u32[]{:S(2)}, u32[]{:S(2)}) collective-permute-start(bf16[72,128,128]{2,1,0:T(8,128)(2,1)} %get-tuple-element.55), channel_id=1, source_target_pairs={{0,24},{8,0},{16,8},{24,16},{1,25},{9,1},{17,9},{25,17},{2,26},{10... | collective-permute-start | bytes 7077896 | tf_op jit(solution)/shard_map/ppermute | solution.py:451
  104.0 28.0 %collective-permute-start.11 = (bf16[16,128,256]{2,1,0:T(8,128)(2,1)}, bf16[16,128,256]{2,1,0:T(8,128)(2,1)}, u32[]{:S(2)}, u32[]{:S(2)}) collective-permute-start(bf16[16,128,256]{2,1,0:T(8,128)(2,1)} %collective-permute-done.10.refs_17_), channel_id=1, source_target_pairs={{0,32},{32,64},{64,96},{96,128},{128,160},{160,192},{192,224},{224... | collective-permute-start | bytes 3145736 | tf_op jit(solution)/shard_map/ppermute | solution.py:459
  107.4 26.3 %collective-permute-start.15 = (bf16[16,128,256]{2,1,0:T(8,128)(2,1)}, bf16[16,128,256]{2,1,0:T(8,128)(2,1)}, u32[]{:S(2)}, u32[]{:S(2)}) collective-permute-start(bf16[16,128,256]{2,1,0:T(8,128)(2,1)} %collective-permute-done.14.refs_16_), channel_id=1, source_target_pairs={{0,224},{32,0},{64,32},{96,64},{128,96},{160,128},{192,160},{224,1... | collective-permute-start | bytes 3145736 | tf_op jit(solution)/shard_map/ppermute | solution.py:461
  108.2 68.2 %collective-permute-start.19 = (bf16[16,128,256]{2,1,0:T(8,128)(2,1)}, bf16[16,128,256]{2,1,0:T(8,128)(2,1)S(1)}, u32[]{:S(2)}, u32[]{:S(2)}) collective-permute-start(bf16[16,128,256]{2,1,0:T(8,128)(2,1)} %collective-permute-done.18.refs_15_), channel_id=1, source_target_pairs={{0,224},{32,0},{64,32},{96,64},{128,96},{160,128},{192,160},{224,1... | collective-permute-start | bytes 3145736 | tf_op jit(solution)/shard_map/ppermute | solution.py:461
  117.0 60.4 %collective-permute-start.22 = (bf16[16,128,256]{2,1,0:T(8,128)(2,1)}, bf16[16,128,256]{2,1,0:T(8,128)(2,1)S(1)}, u32[]{:S(2)}, u32[]{:S(2)}) collective-permute-start(bf16[16,128,256]{2,1,0:T(8,128)(2,1)} %collective-permute-done.21.refs_18_), channel_id=1, source_target_pairs={{0,32},{32,64},{64,96},{96,128},{128,160},{160,192},{192,224},{224... | collective-permute-start | bytes 3145736 | tf_op jit(solution)/shard_map/ppermute | solution.py:459
  132.0 52.0 %collective-permute-start.12 = (bf16[16,128,256]{2,1,0:T(8,128)(2,1)}, bf16[16,128,256]{2,1,0:T(8,128)(2,1)S(1)}, u32[]{:S(2)}, u32[]{:S(2)}) collective-permute-start(bf16[16,128,256]{2,1,0:T(8,128)(2,1)} %collective-permute-done.11.refs_8_), channel_id=1, source_target_pairs={{0,32},{32,64},{64,96},{96,128},{128,160},{160,192},{192,224},{224... | collective-permute-start | bytes 3145736 | tf_op jit(solution)/shard_map/ppermute | solution.py:459
  133.7 51.3 %collective-permute-start.16 = (bf16[16,128,256]{2,1,0:T(8,128)(2,1)}, bf16[16,128,256]{2,1,0:T(8,128)(2,1)}, u32[]{:S(2)}, u32[]{:S(2)}) collective-permute-start(bf16[16,128,256]{2,1,0:T(8,128)(2,1)} %collective-permute-done.15.refs_7_), channel_id=1, source_target_pairs={{0,224},{32,0},{64,32},{96,64},{128,96},{160,128},{192,160},{224,1... | collective-permute-start | bytes 3145736 | tf_op jit(solution)/shard_map/ppermute | solution.py:461
  194.2 19.7 %collective-permute-start.24 = (f32[4,64,256]{2,1,0:T(8,128)S(1)}, f32[4,64,256]{2,1,0:T(8,128)S(1)}, u32[]{:S(2)}, u32[]{:S(2)}) collective-permute-start(f32[4,64,256]{2,1,0:T(8,128)S(1)} %get-tuple-element.68), channel_id=1, source_target_pairs={{0,16},{8,24},{16,0},{24,8},{1,17},{9,25},{17,1},{25,9},{2,18},{10... | collective-permute-start | bytes 786440 | tf_op jit(solution)/shard_map/ppermute | solution.py:519
  195.4 21.4 %collective-permute-start.25 = (f32[4,64,256]{2,1,0:T(8,128)S(1)}, f32[4,64,256]{2,1,0:T(8,128)S(1)}, u32[]{:S(2)}, u32[]{:S(2)}) collective-permute-start(f32[4,64,256]{2,1,0:T(8,128)S(1)} %get-tuple-element.69), channel_id=1, source_target_pairs={{0,4},{2,6},{4,0},{6,2},{1,5},{3,7},{5,1},{7,3},{8,12},{10,14},{12... | collective-permute-start | bytes 786440 | tf_op jit(solution)/shard_map/ppermute | solution.py:519
  198.2 23.1 %collective-permute-start.26 = (f32[4,64,256]{2,1,0:T(8,128)S(1)}, f32[4,64,256]{2,1,0:T(8,128)S(1)}, u32[]{:S(2)}, u32[]{:S(2)}) collective-permute-start(f32[4,64,256]{2,1,0:T(8,128)S(1)} %get-tuple-element.70), channel_id=1, source_target_pairs={{0,8},{8,16},{16,24},{24,0},{1,9},{9,17},{17,25},{25,1},{2,10},{10... | collective-permute-start | bytes 786440 | tf_op jit(solution)/shard_map/ppermute | solution.py:519
  221.9 12.0 %collective-permute-start.30 = (f32[64,256]{1,0:T(8,128)S(1)}, f32[64,256]{1,0:T(8,128)S(1)}, u32[]{:S(2)}, u32[]{:S(2)}) collective-permute-start(f32[64,256]{1,0:T(8,128)S(1)} %get-tuple-element.76), channel_id=1, source_target_pairs={{0,4},{2,6},{4,0},{6,2},{1,5},{3,7},{5,1},{7,3},{8,12},{10,14},{12... | collective-permute-start | bytes 196616 | tf_op jit(solution)/shard_map/ppermute | solution.py:519
  (21 other events, 186.7 us)

commit v3 on v2

--- a/solution.py
+++ b/solution.py
@@ -234,23 +234,21 @@
 
 
 def add_up_kernel(*refs):
-    outs = refs[2 * NX :]
-    for side in range(2):
-        ins = refs[side : 2 * NX : 2]
-        for r in range(NX):
-            outs[side * NX + r][...] = (ins[0][r] + ins[1][r]) + (ins[2][r] + ins[3][r])
-
-
-def in_vmem(kernel, args, shape):
+    ins, outs = refs[:NX], refs[NX:]
+    for r in range(NX):
+        outs[r][...] = (ins[0][r] + ins[1][r]) + (ins[2][r] + ins[3][r])
+
+
+def in_vmem(kernel, args, shape, n):
     vm = pl.BlockSpec(memory_space=pltpu.VMEM)
     out = pl.pallas_call(
         kernel,
-        out_shape=[jax.ShapeDtypeStruct(shape, jnp.float32)] * (2 * NX),
+        out_shape=[jax.ShapeDtypeStruct(shape, jnp.float32)] * n,
         in_specs=[vm] * len(args),
-        out_specs=[vm] * (2 * NX),
+        out_specs=[vm] * n,
         compiler_params=pltpu.CompilerParams(vmem_limit_bytes=16 << 20),
     )(*args)
-    return out[:NX], out[NX:]
+    return out
 
 
 def in_turn(top, bottom):
@@ -286,11 +284,12 @@
 
 
 def spread(mine, theirs):
-    return in_vmem(spread_kernel, (mine, theirs), (NY, BS // 2, K))
-
-
-def add_up(top, bottom):
-    return in_vmem(add_up_kernel, in_turn(top, bottom), (BS // 2, K))
+    out = in_vmem(spread_kernel, (mine, theirs), (NY, BS // 2, K), 2 * NX)
+    return out[:NX], out[NX:]
+
+
+def add_up(side):
+    return in_vmem(add_up_kernel, [side[r] for r in (2, 1, 3, 0)], (BS // 2, K), NX)
 
 
 def factor_block(d):
@@ -518,7 +517,7 @@
             for axis, side in zip(axes, moved):
                 side[r] = lax.ppermute(side[r], axis, ring(NX, r))
         if axes[0] == "x":
-            parts = add_up(*moved)
+            parts = add_up(moved[0]), add_up(moved[1])
     gram, image_t = local_gram(*moved)
     plane = ("x", "y", "core")
     n_plane = NX * NY * NC

time: 294 us -> 291 us (0.990)
  waiting for transfers between devices: 121 us -> 118 us
  transfers between devices with their start and end apart: 33 -> 33, of which waited for: 17 -> 15; matrix products, arithmetic and copies ran while one was open for 3% -> 3% of each run, Pallas kernels for 12% -> 12%
where the time goes in v3:
time: 291 us; the launch traced here: 288 us
  waiting for transfers between devices  118 us (41%)
  starting transfers between devices  61.5 us (21%)
  Pallas kernels  51.7 us (18%)
  blocking collectives  39.3 us (14%)
  local copies, waits for them, and re-layouts  10.4 us (4%)
  other arithmetic  5.43 us (2%)
    ppermute x12, starting transfers between devices, one_device(): side[r] = lax.ppermute(side[r], axis, ring(NX, r))  35.2 us
    ppermute x5, waiting for transfers between devices, one_device(): fwd[step][h] = lax.ppermute(fwd[step - 1][h], 'z', ring(NZ, 1))  34.9 us
    ppermute x3, waiting for transfers between devices, one_device(): vals[dx] = lax.ppermute(vals[dx], 'x', ring(NX, dx))  28.7 us
    pallas_call x3, Pallas kernels, products(): pl.pallas_call(functools.partial(products_kernel, ds, halves, window, fir...  22.4 us
    ppermute x5, waiting for transfers between devices, one_device(): bwd[step][h] = lax.ppermute(bwd[step - 1][h], 'z', ring(NZ, -1))  22.1 us
    all_to_all x1, blocking collectives, one_device(): part = jnp.sum(lax.all_to_all(gram, plane, 0, 0, tiled=True), axis=0)  14.5 us
    ppermute x2, waiting for transfers between devices, one_device(): fwd = {1: [lax.ppermute(blocks[h], 'z', ring(NZ, 1)) for h in range(2)]}  13.2 us
    pallas_call x2, Pallas kernels, pack(): pl.pallas_call(functools.partial(pack_kernel, n), out_shape=[jax.ShapeDty...  12.8 us
  transfers between devices with their start and end apart: 33, of which 15 were waited for; matrix products, arithmetic and copies ran while one was open for 3% of the time, Pallas kernels for 12%

profile of v3, /device:TPU:2, one launch (start us, length us, event | category | flops | bytes accessed | tf_op | source)
XLA Modules:
  0.0 288.4 jit_solution(15629878897735555975)
XLA Ops:
  10.7 4.0 %collective-permute-start.13 = (bf16[16,128,256]{2,1,0:T(8,128)(2,1)}, bf16[16,128,256]{2,1,0:T(8,128)(2,1)}, u32[]{:S(2)}, u32[]{:S(2)}) collective-permute-start(bf16[16,128,256]{2,1,0:T(8,128)(2,1)} %get-tuple-element.57), channel_id=1, source_target_pairs={{0,224},{32,0},{64,32},{96,64},{128,96},{160,128},{192,160},{224,1... | collective-permute-start | bytes 3145736 | tf_op jit(solution)/shard_map/ppermute | solution.py:430
  20.2 3.4 %conditional.1 = (bf16[24,128,128]{2,1,0:T(8,128)(2,1)S(1)}, bf16[24,128,128]{2,1,0:T(8,128)(2,1)}, bf16[24,128,128]{2,1,0:T(8,128)(2,1)}, bf16[24,128,128]{2,1,0:T(8,128)(2,1)}) conditional(s32[]{:T(128)} %convert_element_type.19, () %tuple.18, (s32[4,96]{1,0:T(4,128)S(1)}, bf16[256,128,128]{2,1,0:T(8,128)(2,1)}) %tuple.35), branch_computations={%region_10.11_spmd, %region_11.12_spmd} | conditional | flops 4384 | bytes 15746712 | solution.py:505
  25.7 13.1 %collective-permute-done.9.refs_13_ = bf16[16,128,256]{2,1,0:T(8,128)(2,1)S(1)} collective-permute-done((bf16[16,128,256]{2,1,0:T(8,128)(2,1)}, bf16[16,128,256]{2,1,0:T(8,128)(2,1)S(1)}, u32[]{:S(2)}, u32[]{:S(2)}) %collective-permute-start.9) | collective-permute-done | bytes 1048608 | tf_op jit(solution)/shard_map/ppermute | solution.py:429
  38.8 3.4 %collective-permute-start.14 = (bf16[16,128,256]{2,1,0:T(8,128)(2,1)}, bf16[16,128,256]{2,1,0:T(8,128)(2,1)}, u32[]{:S(2)}, u32[]{:S(2)}) collective-permute-start(bf16[16,128,256]{2,1,0:T(8,128)(2,1)} %collective-permute-done.13.refs_12_), channel_id=1, source_target_pairs={{0,224},{32,0},{64,32},{96,64},{128,96},{160,128},{192,160},{224,1... | collective-permute-start | bytes 3145736 | tf_op jit(solution)/shard_map/ppermute | solution.py:460
  42.3 9.6 %shard_map.60 = (bf16[72,128,128]{2,1,0:T(8,128)(2,1)}, bf16[72,128,128]{2,1,0:T(8,128)(2,1)}, bf16[72,128,128]{2,1,0:T(8,128)(2,1)}) custom-call(s32[216]{0:T(256)S(1)} %reshape.1294.index, bf16[256,128,128]{2,1,0:T(8,128)(2,1)} %bitcast.45), custom_call_target="tpu_custom_call" | custom-call | bytes 14155776 | tf_op jit(solution)/shard_map/pallas_call | solution.py:87
  52.1 9.0 %collective-permute-done.17.refs_11_ = bf16[16,128,256]{2,1,0:T(8,128)(2,1)} collective-permute-done((bf16[16,128,256]{2,1,0:T(8,128)(2,1)}, bf16[16,128,256]{2,1,0:T(8,128)(2,1)}, u32[]{:S(2)}, u32[]{:S(2)}) %collective-permute-start.17) | collective-permute-done | bytes 1048608 | tf_op jit(solution)/shard_map/ppermute | solution.py:430
  61.4 3.6 %collective-permute-start.18 = (bf16[16,128,256]{2,1,0:T(8,128)(2,1)}, bf16[16,128,256]{2,1,0:T(8,128)(2,1)}, u32[]{:S(2)}, u32[]{:S(2)}) collective-permute-start(bf16[16,128,256]{2,1,0:T(8,128)(2,1)} %collective-permute-done.17.refs_11_), channel_id=1, source_target_pairs={{0,224},{32,0},{64,32},{96,64},{128,96},{160,128},{192,160},{224,1... | collective-permute-start | bytes 3145736 | tf_op jit(solution)/shard_map/ppermute | solution.py:460
  65.0 17.2 %collective-permute-done.10.refs_17_ = bf16[16,128,256]{2,1,0:T(8,128)(2,1)} collective-permute-done((bf16[16,128,256]{2,1,0:T(8,128)(2,1)S(1)}, bf16[16,128,256]{2,1,0:T(8,128)(2,1)}, u32[]{:S(2)}, u32[]{:S(2)}) %collective-permute-start.10) | collective-permute-done | bytes 1048608 | tf_op jit(solution)/shard_map/ppermute | solution.py:458
  84.9 19.1 %collective-permute-done.18.refs_15_ = bf16[16,128,256]{2,1,0:T(8,128)(2,1)} collective-permute-done((bf16[16,128,256]{2,1,0:T(8,128)(2,1)}, bf16[16,128,256]{2,1,0:T(8,128)(2,1)}, u32[]{:S(2)}, u32[]{:S(2)}) %collective-permute-start.18) | collective-permute-done | bytes 1048608 | tf_op jit(solution)/shard_map/ppermute | solution.py:460
  110.3 6.7 %collective-permute-done.7.refs_4_ = bf16[72,128,128]{2,1,0:T(8,128)(2,1)} collective-permute-done((bf16[72,128,128]{2,1,0:T(8,128)(2,1)}, bf16[72,128,128]{2,1,0:T(8,128)(2,1)}, u32[]{:S(2)}, u32[]{:S(2)}) %collective-permute-start.7) | collective-permute-done | bytes 2359328 | tf_op jit(solution)/shard_map/ppermute | solution.py:450
  117.4 14.6 %collective-permute-done.11.refs_8_ = bf16[16,128,256]{2,1,0:T(8,128)(2,1)} collective-permute-done((bf16[16,128,256]{2,1,0:T(8,128)(2,1)}, bf16[16,128,256]{2,1,0:T(8,128)(2,1)}, u32[]{:S(2)}, u32[]{:S(2)}) %collective-permute-start.11) | collective-permute-done | bytes 1048608 | tf_op jit(solution)/shard_map/ppermute | solution.py:458
  140.8 22.0 %collective-permute-done.8.refs_5_ = bf16[72,128,128]{2,1,0:T(8,128)(2,1)} collective-permute-done((bf16[72,128,128]{2,1,0:T(8,128)(2,1)}, bf16[72,128,128]{2,1,0:T(8,128)(2,1)}, u32[]{:S(2)}, u32[]{:S(2)}) %collective-permute-start.8) | collective-permute-done | bytes 2359328 | tf_op jit(solution)/shard_map/ppermute | solution.py:450
  162.7 13.7 %shard_map.61 = (f32[16,128,256]{2,1,0:T(8,128)S(1)}, f32[16,128,256]{2,1,0:T(8,128)S(1)}) custom-call(s32[768]{0:T(1024)S(1)} %broadcast_add_fusion.refs_0_, s32[17]{0:T(128)S(1)} %pad_add_fusion.1.refs_1_, bf16[72,128,128]{2,1,0:T(8,128)(2,1)} %copy-done, bf16[72,128,128]{2,1,0:T(8,128)(2,1)} %copy-done.2, ...), custom_call_target="tpu_custom_call" | custom-call | flops 838860800 | bytes 23068672 | tf_op jit(solution)/shard_map/pallas_call | solution.py:196
  178.7 5.3 %shard_map.62 = (f32[16,128,256]{2,1,0:T(8,128)S(1)}, f32[16,128,256]{2,1,0:T(8,128)S(1)}) custom-call(s32[768]{0:T(1024)S(1)} %broadcast_add_fusion.refs_0_, s32[17]{0:T(128)S(1)} %pad_add_fusion.1.refs_1_, bf16[72,128,128]{2,1,0:T(8,128)(2,1)S(1)} %copy-done.1, ...), custom_call_target="tpu_custom_call", output_to_operand_aliasing={{0}: (10, {}), {1}: (11, {})} | custom-call | flops 335544320 | bytes 8912896 | tf_op jit(solution)/shard_map/pallas_call | solution.py:196
  186.2 3.4 %shard_map.63 = (f32[16,128,256]{2,1,0:T(8,128)S(1)}, f32[16,128,256]{2,1,0:T(8,128)S(1)}) custom-call(s32[768]{0:T(1024)S(1)} %broadcast_add_fusion.refs_0_, s32[17]{0:T(128)S(1)} %pad_add_fusion.1.refs_1_, bf16[72,128,128]{2,1,0:T(8,128)(2,1)S(1)} %copy-done.1, bf16[72,128,128]{2,1,0:T(8,128)(2,1)S(1)} %copy-done.3, ...), custom_call_target="tpu_custom_call", output_to_operand_aliasing={{0}: (8, {}), {1}: (9, {})} | custom-call | flops 167772160 | bytes 3670016 | tf_op jit(solution)/shard_map/pallas_call | solution.py:196
  189.8 4.1 %collective-permute-done.23.theirs = f32[16,128,256]{2,1,0:T(8,128)S(1)} collective-permute-done((f32[16,128,256]{2,1,0:T(8,128)S(1)}, f32[16,128,256]{2,1,0:T(8,128)S(1)}, u32[]{:S(2)}, u32[]{:S(2)}) %collective-permute-start.23) | collective-permute-done | bytes 2097184 | tf_op jit(solution)/shard_map/ppermute | solution.py:513
  194.2 3.6 %collective-permute-start.28 = (f32[4,64,256]{2,1,0:T(8,128)S(1)}, f32[4,64,256]{2,1,0:T(8,128)S(1)}, u32[]{:S(2)}, u32[]{:S(2)}) collective-permute-start(f32[4,64,256]{2,1,0:T(8,128)S(1)} %get-tuple-element.73), channel_id=1, source_target_pairs={{0,4},{2,6},{4,0},{6,2},{1,5},{3,7},{5,1},{7,3},{8,12},{10,14},{12... | collective-permute-start | bytes 786440 | tf_op jit(solution)/shard_map/ppermute | solution.py:518
  201.4 14.9 %collective-permute-start.25 = (f32[4,64,256]{2,1,0:T(8,128)S(1)}, f32[4,64,256]{2,1,0:T(8,128)S(1)}, u32[]{:S(2)}, u32[]{:S(2)}) collective-permute-start(f32[4,64,256]{2,1,0:T(8,128)S(1)} %get-tuple-element.69), channel_id=1, source_target_pairs={{0,8},{8,16},{16,24},{24,0},{1,9},{9,17},{17,25},{25,1},{2,10},{10... | collective-permute-start | bytes 786440 | tf_op jit(solution)/shard_map/ppermute | solution.py:518
  220.4 5.5 %collective-permute-start.33 = (f32[64,256]{1,0:T(8,128)S(1)}, f32[64,256]{1,0:T(8,128)S(1)}, u32[]{:S(2)}, u32[]{:S(2)}) collective-permute-start(f32[64,256]{1,0:T(8,128)S(1)} %get-tuple-element.79), channel_id=1, source_target_pairs={{0,8},{8,16},{16,24},{24,0},{1,9},{9,17},{17,25},{25,1},{2,10},{10... | collective-permute-start | bytes 196616 | tf_op jit(solution)/shard_map/ppermute | solution.py:518
  226.0 3.4 %collective-permute-done.25.refs_1_ = f32[4,64,256]{2,1,0:T(8,128)S(1)} collective-permute-done((f32[4,64,256]{2,1,0:T(8,128)S(1)}, f32[4,64,256]{2,1,0:T(8,128)S(1)}, u32[]{:S(2)}, u32[]{:S(2)}) %collective-permute-start.25) | collective-permute-done | bytes 262176 | tf_op jit(solution)/shard_map/ppermute | solution.py:518
  236.9 14.5 %all_to_all.15 = f32[32,8,256]{2,1,0:T(8,128)S(1)} all-to-all(f32[32,8,256]{2,1,0:T(8,128)S(1)} %bitcast.43), channel_id=1, replica_groups=mesh['z'=8,'x'=4,'y'=4,'core'=2] {'x','y','core'}, dimensions={0} | all-to-all | bytes 524288 | tf_op jit(solution)/shard_map/all_to_all | solution.py:526
  251.5 12.2 %all_to_all.16 = f32[8,8,256]{2,1,0:T(8,128)S(1)} all-to-all(f32[8,8,256]{2,1,0:T(8,128)S(1)} %broadcast_in_dim.106), channel_id=1, replica_groups=mesh['z'=8,'x'=4,'y'=4,'core'=2] {'z'}, dimensions={0} | all-to-all | bytes 131072 | tf_op jit(solution)/shard_map/all_to_all | solution.py:528
  263.7 12.6 %all_to_all.17 = f32[32,8,256]{2,1,0:T(8,128)} all-to-all(f32[32,8,256]{2,1,0:T(8,128)S(1)} %broadcast_in_dim.107), channel_id=1, replica_groups=mesh['z'=8,'x'=4,'y'=4,'core'=2] {'x','y','core'}, dimensions={0} | all-to-all | bytes 524288 | tf_op jit(solution)/shard_map/all_to_all | solution.py:530
  276.3 12.1 %factor.1 = (f32[256,256]{1,0:T(8,128)}, f32[128,256]{1,0:T(8,128)}) custom-call(f32[256,256]{1,0:T(8,128)} %bitcast.49, f32[256,128]{1,0:T(8,128)} %copy-done.8), custom_call_target="tpu_custom_call" | custom-call | tf_op jit(solution)/shard_map/factor/pallas_call | solution.py:384
  (126 shorter events, 59.1 us)
Async XLA Ops:
  1.5 13.8 %collective-permute-start.3 = (s32[2,128]{1,0:T(2,128)S(1)}, s32[2,128]{1,0:T(2,128)S(1)}, u32[]{:S(2)}, u32[]{:S(2)}) collective-permute-start(s32[2,128]{1,0:T(2,128)S(1)} %reshape_reshape.3.x_ref), channel_id=1, source_target_pairs={{0,8},{8,16},{16,24},{24,0},{1,9},{9,17},{17,25},{25,1},{2,10},{10... | collective-permute-start | bytes 3080 | tf_op jit(solution)/shard_map/ppermute | solution.py:446
  8.7 30.2 %collective-permute-start.9 = (bf16[16,128,256]{2,1,0:T(8,128)(2,1)}, bf16[16,128,256]{2,1,0:T(8,128)(2,1)S(1)}, u32[]{:S(2)}, u32[]{:S(2)}) collective-permute-start(bf16[16,128,256]{2,1,0:T(8,128)(2,1)} %get-tuple-element.56), channel_id=1, source_target_pairs={{0,32},{32,64},{64,96},{96,128},{128,160},{160,192},{192,224},{224... | collective-permute-start | bytes 3145736 | tf_op jit(solution)/shard_map/ppermute | solution.py:429
  10.7 28.2 %collective-permute-start.13 = (bf16[16,128,256]{2,1,0:T(8,128)(2,1)}, bf16[16,128,256]{2,1,0:T(8,128)(2,1)}, u32[]{:S(2)}, u32[]{:S(2)}) collective-permute-start(bf16[16,128,256]{2,1,0:T(8,128)(2,1)} %get-tuple-element.57), channel_id=1, source_target_pairs={{0,224},{32,0},{64,32},{96,64},{128,96},{160,128},{192,160},{224,1... | collective-permute-start | bytes 3145736 | tf_op jit(solution)/shard_map/ppermute | solution.py:430
  23.7 37.4 %collective-permute-start.17 = (bf16[16,128,256]{2,1,0:T(8,128)(2,1)}, bf16[16,128,256]{2,1,0:T(8,128)(2,1)}, u32[]{:S(2)}, u32[]{:S(2)}) collective-permute-start(bf16[16,128,256]{2,1,0:T(8,128)(2,1)} %get-tuple-element.56), channel_id=1, source_target_pairs={{0,224},{32,0},{64,32},{96,64},{128,96},{160,128},{192,160},{224,1... | collective-permute-start | bytes 3145736 | tf_op jit(solution)/shard_map/ppermute | solution.py:430
  25.6 35.8 %collective-permute-start.20 = (bf16[16,128,256]{2,1,0:T(8,128)(2,1)}, bf16[16,128,256]{2,1,0:T(8,128)(2,1)}, u32[]{:S(2)}, u32[]{:S(2)}) collective-permute-start(bf16[16,128,256]{2,1,0:T(8,128)(2,1)} %get-tuple-element.57), channel_id=1, source_target_pairs={{0,32},{32,64},{64,96},{96,128},{128,160},{160,192},{192,224},{224... | collective-permute-start | bytes 3145736 | tf_op jit(solution)/shard_map/ppermute | solution.py:429
  38.8 43.4 %collective-permute-start.10 = (bf16[16,128,256]{2,1,0:T(8,128)(2,1)S(1)}, bf16[16,128,256]{2,1,0:T(8,128)(2,1)}, u32[]{:S(2)}, u32[]{:S(2)}) collective-permute-start(bf16[16,128,256]{2,1,0:T(8,128)(2,1)S(1)} %collective-permute-done.9.refs_13_), channel_id=1, source_target_pairs={{0,32},{32,64},{64,96},{96,128},{128,160},{160,192},{192,224},{224... | collective-permute-start | bytes 3145736 | tf_op jit(solution)/shard_map/ppermute | solution.py:458
  38.8 44.7 %collective-permute-start.14 = (bf16[16,128,256]{2,1,0:T(8,128)(2,1)}, bf16[16,128,256]{2,1,0:T(8,128)(2,1)}, u32[]{:S(2)}, u32[]{:S(2)}) collective-permute-start(bf16[16,128,256]{2,1,0:T(8,128)(2,1)} %collective-permute-done.13.refs_12_), channel_id=1, source_target_pairs={{0,224},{32,0},{64,32},{96,64},{128,96},{160,128},{192,160},{224,1... | collective-permute-start | bytes 3145736 | tf_op jit(solution)/shard_map/ppermute | solution.py:460
  52.0 56.2 %collective-permute-start.6 = (bf16[72,128,128]{2,1,0:T(8,128)(2,1)}, bf16[72,128,128]{2,1,0:T(8,128)(2,1)S(1)}, u32[]{:S(2)}, u32[]{:S(2)}) collective-permute-start(bf16[72,128,128]{2,1,0:T(8,128)(2,1)} %get-tuple-element.53), channel_id=1, source_target_pairs={{0,8},{8,16},{16,24},{24,0},{1,9},{9,17},{17,25},{25,1},{2,10},{10... | collective-permute-start | bytes 7077896 | tf_op jit(solution)/shard_map/ppermute | solution.py:450
  61.0 56.0 %collective-permute-start.7 = (bf16[72,128,128]{2,1,0:T(8,128)(2,1)}, bf16[72,128,128]{2,1,0:T(8,128)(2,1)}, u32[]{:S(2)}, u32[]{:S(2)}) collective-permute-start(bf16[72,128,128]{2,1,0:T(8,128)(2,1)} %get-tuple-element.54), channel_id=1, source_target_pairs={{0,16},{8,24},{16,0},{24,8},{1,17},{9,25},{17,1},{25,9},{2,18},{10... | collective-permute-start | bytes 7077896 | tf_op jit(solution)/shard_map/ppermute | solution.py:450
  61.4 42.6 %collective-permute-start.18 = (bf16[16,128,256]{2,1,0:T(8,128)(2,1)}, bf16[16,128,256]{2,1,0:T(8,128)(2,1)}, u32[]{:S(2)}, u32[]{:S(2)}) collective-permute-start(bf16[16,128,256]{2,1,0:T(8,128)(2,1)} %collective-permute-done.17.refs_11_), channel_id=1, source_target_pairs={{0,224},{32,0},{64,32},{96,64},{128,96},{160,128},{192,160},{224,1... | collective-permute-start | bytes 3145736 | tf_op jit(solution)/shard_map/ppermute | solution.py:460
  82.2 25.2 %collective-permute-start.21 = (bf16[16,128,256]{2,1,0:T(8,128)(2,1)}, bf16[16,128,256]{2,1,0:T(8,128)(2,1)}, u32[]{:S(2)}, u32[]{:S(2)}) collective-permute-start(bf16[16,128,256]{2,1,0:T(8,128)(2,1)} %collective-permute-done.20.refs_14_), channel_id=1, source_target_pairs={{0,32},{32,64},{64,96},{96,128},{128,160},{160,192},{192,224},{224... | collective-permute-start | bytes 3145736 | tf_op jit(solution)/shard_map/ppermute | solution.py:458
  83.5 79.2 %collective-permute-start.8 = (bf16[72,128,128]{2,1,0:T(8,128)(2,1)}, bf16[72,128,128]{2,1,0:T(8,128)(2,1)}, u32[]{:S(2)}, u32[]{:S(2)}) collective-permute-start(bf16[72,128,128]{2,1,0:T(8,128)(2,1)} %get-tuple-element.55), channel_id=1, source_target_pairs={{0,24},{8,0},{16,8},{24,16},{1,25},{9,1},{17,9},{25,17},{2,26},{10... | collective-permute-start | bytes 7077896 | tf_op jit(solution)/shard_map/ppermute | solution.py:450
  104.0 28.0 %collective-permute-start.11 = (bf16[16,128,256]{2,1,0:T(8,128)(2,1)}, bf16[16,128,256]{2,1,0:T(8,128)(2,1)}, u32[]{:S(2)}, u32[]{:S(2)}) collective-permute-start(bf16[16,128,256]{2,1,0:T(8,128)(2,1)} %collective-permute-done.10.refs_17_), channel_id=1, source_target_pairs={{0,32},{32,64},{64,96},{96,128},{128,160},{160,192},{192,224},{224... | collective-permute-start | bytes 3145736 | tf_op jit(solution)/shard_map/ppermute | solution.py:458
  107.4 26.3 %collective-permute-start.15 = (bf16[16,128,256]{2,1,0:T(8,128)(2,1)}, bf16[16,128,256]{2,1,0:T(8,128)(2,1)}, u32[]{:S(2)}, u32[]{:S(2)}) collective-permute-start(bf16[16,128,256]{2,1,0:T(8,128)(2,1)} %collective-permute-done.14.refs_16_), channel_id=1, source_target_pairs={{0,224},{32,0},{64,32},{96,64},{128,96},{160,128},{192,160},{224,1... | collective-permute-start | bytes 3145736 | tf_op jit(solution)/shard_map/ppermute | solution.py:460
  108.2 68.2 %collective-permute-start.19 = (bf16[16,128,256]{2,1,0:T(8,128)(2,1)}, bf16[16,128,256]{2,1,0:T(8,128)(2,1)S(1)}, u32[]{:S(2)}, u32[]{:S(2)}) collective-permute-start(bf16[16,128,256]{2,1,0:T(8,128)(2,1)} %collective-permute-done.18.refs_15_), channel_id=1, source_target_pairs={{0,224},{32,0},{64,32},{96,64},{128,96},{160,128},{192,160},{224,1... | collective-permute-start | bytes 3145736 | tf_op jit(solution)/shard_map/ppermute | solution.py:460
  117.0 60.4 %collective-permute-start.22 = (bf16[16,128,256]{2,1,0:T(8,128)(2,1)}, bf16[16,128,256]{2,1,0:T(8,128)(2,1)S(1)}, u32[]{:S(2)}, u32[]{:S(2)}) collective-permute-start(bf16[16,128,256]{2,1,0:T(8,128)(2,1)} %collective-permute-done.21.refs_18_), channel_id=1, source_target_pairs={{0,32},{32,64},{64,96},{96,128},{128,160},{160,192},{192,224},{224... | collective-permute-start | bytes 3145736 | tf_op jit(solution)/shard_map/ppermute | solution.py:458
  132.0 52.0 %collective-permute-start.12 = (bf16[16,128,256]{2,1,0:T(8,128)(2,1)}, bf16[16,128,256]{2,1,0:T(8,128)(2,1)S(1)}, u32[]{:S(2)}, u32[]{:S(2)}) collective-permute-start(bf16[16,128,256]{2,1,0:T(8,128)(2,1)} %collective-permute-done.11.refs_8_), channel_id=1, source_target_pairs={{0,32},{32,64},{64,96},{96,128},{128,160},{160,192},{192,224},{224... | collective-permute-start | bytes 3145736 | tf_op jit(solution)/shard_map/ppermute | solution.py:458
  133.7 51.3 %collective-permute-start.16 = (bf16[16,128,256]{2,1,0:T(8,128)(2,1)}, bf16[16,128,256]{2,1,0:T(8,128)(2,1)}, u32[]{:S(2)}, u32[]{:S(2)}) collective-permute-start(bf16[16,128,256]{2,1,0:T(8,128)(2,1)} %collective-permute-done.15.refs_7_), channel_id=1, source_target_pairs={{0,224},{32,0},{64,32},{96,64},{128,96},{160,128},{192,160},{224,1... | collective-permute-start | bytes 3145736 | tf_op jit(solution)/shard_map/ppermute | solution.py:460
  194.2 22.2 %collective-permute-start.28 = (f32[4,64,256]{2,1,0:T(8,128)S(1)}, f32[4,64,256]{2,1,0:T(8,128)S(1)}, u32[]{:S(2)}, u32[]{:S(2)}) collective-permute-start(f32[4,64,256]{2,1,0:T(8,128)S(1)} %get-tuple-element.73), channel_id=1, source_target_pairs={{0,4},{2,6},{4,0},{6,2},{1,5},{3,7},{5,1},{7,3},{8,12},{10,14},{12... | collective-permute-start | bytes 786440 | tf_op jit(solution)/shard_map/ppermute | solution.py:518
  197.8 21.7 %collective-permute-start.29 = (f32[4,64,256]{2,1,0:T(8,128)S(1)}, f32[4,64,256]{2,1,0:T(8,128)S(1)}, u32[]{:S(2)}, u32[]{:S(2)}) collective-permute-start(f32[4,64,256]{2,1,0:T(8,128)S(1)} %get-tuple-element.74), channel_id=1, source_target_pairs={{0,2},{2,4},{4,6},{6,0},{1,3},{3,5},{5,7},{7,1},{8,10},{10,12},{12... | collective-permute-start | bytes 786440 | tf_op jit(solution)/shard_map/ppermute | solution.py:518
  197.8 21.7 %collective-permute-start.30 = (f32[4,64,256]{2,1,0:T(8,128)S(1)}, f32[4,64,256]{2,1,0:T(8,128)S(1)}, u32[]{:S(2)}, u32[]{:S(2)}) collective-permute-start(f32[4,64,256]{2,1,0:T(8,128)S(1)} %get-tuple-element.75), channel_id=1, source_target_pairs={{0,6},{2,0},{4,2},{6,4},{1,7},{3,1},{5,3},{7,5},{8,14},{10,8},{12,... | collective-permute-start | bytes 786440 | tf_op jit(solution)/shard_map/ppermute | solution.py:518
  201.0 24.8 %collective-permute-start.24 = (f32[4,64,256]{2,1,0:T(8,128)S(1)}, f32[4,64,256]{2,1,0:T(8,128)S(1)}, u32[]{:S(2)}, u32[]{:S(2)}) collective-permute-start(f32[4,64,256]{2,1,0:T(8,128)S(1)} %get-tuple-element.68), channel_id=1, source_target_pairs={{0,16},{8,24},{16,0},{24,8},{1,17},{9,25},{17,1},{25,9},{2,18},{10... | collective-permute-start | bytes 786440 | tf_op jit(solution)/shard_map/ppermute | solution.py:518
  201.4 28.0 %collective-permute-start.25 = (f32[4,64,256]{2,1,0:T(8,128)S(1)}, f32[4,64,256]{2,1,0:T(8,128)S(1)}, u32[]{:S(2)}, u32[]{:S(2)}) collective-permute-start(f32[4,64,256]{2,1,0:T(8,128)S(1)} %get-tuple-element.69), channel_id=1, source_target_pairs={{0,8},{8,16},{16,24},{24,0},{1,9},{9,17},{17,25},{25,1},{2,10},{10... | collective-permute-start | bytes 786440 | tf_op jit(solution)/shard_map/ppermute | solution.py:518
  216.3 13.1 %collective-permute-start.26 = (f32[4,64,256]{2,1,0:T(8,128)S(1)}, f32[4,64,256]{2,1,0:T(8,128)S(1)}, u32[]{:S(2)}, u32[]{:S(2)}) collective-permute-start(f32[4,64,256]{2,1,0:T(8,128)S(1)} %get-tuple-element.70), channel_id=1, source_target_pairs={{0,24},{8,0},{16,8},{24,16},{1,25},{9,1},{17,9},{25,17},{2,26},{10... | collective-permute-start | bytes 786440 | tf_op jit(solution)/shard_map/ppermute | solution.py:518
  (21 other events, 200.3 us)
